TPU v7x, 512 devices: a whole 4x8x8 slice. The times are simulated.
512 devices in a mesh: band: 16 (over z_hi, x), grid: 32 (over z_lo, y, core).
Axes of the slice: x: 4, y: 8, z: 8 (z_hi: 4, z_lo: 2; z = z_hi * 2 + z_lo), core: 2. Of those that a mesh axis runs over, the one named last changes fastest.
Arguments:
- valence: bfloat16 [256, 96, 9216], P('band', 'grid'), may hold values from -6 to 6
- conduction: bfloat16 [128, 96, 9216], P('band', 'grid'), may hold values from -6 to 6
- screened: bfloat16 [6144, 6144], P('grid'), may hold values from -0.0007324219 to 0.0007324219
- blocks: int32 [2], replicated, may hold values from 0 to 31
- gsphere: int32 [6144], P('grid'), may hold values from 0 to 1023, as said below
Outputs:
- kernel: float32 [16, 64, 64], P('band', 'grid')
Inputs may be any that keep to these rules, and one draw needn't show every extreme that they name: `gsphere`: distinct within each aligned block of 192 entries.
All inputs are finite; a program needn't handle non-finite values.
Results may differ from a plain program's by a relative error of at most 0.0093.
Values may be sent and summed in bfloat16 or wider, within the bound.
A program may use at most 64 MiB of HBM per device.

v0:
```python
import math

import jax
import jax.numpy as jnp
from jax import lax
from jax.sharding import Mesh
from jax.sharding import PartitionSpec as P

GRID_N = 96
KF = 32
BLK = 8
BAND = ("band_0", "band_1")


def from_root(x, axes, root):
    x = jnp.where(lax.axis_index(axes) == root, x, jnp.zeros_like(x))
    for axis in axes:
        x = lax.psum(x, axis)
    return x


def broadcast(x, axis, root):
    return lax.dynamic_index_in_dim(lax.all_gather(x, axis), root, 0, keepdims=False)


def in_blocks(x, dim, peers):
    shape = x.shape
    blocks = x.reshape(*shape[:dim], peers, shape[dim] // peers, *shape[dim + 1 :])
    return jnp.moveaxis(blocks, dim, 0)


def summed_on_arrival(x, axis, dim):
    blocks = in_blocks(x, dim, lax.axis_size(axis))
    arrived = lax.all_to_all(blocks, axis, split_axis=0, concat_axis=0, tiled=True)
    return arrived.sum(axis=0)


def fourier_parts(length, kept):
    positions = jnp.arange(length, dtype=jnp.int32)
    freqs = jnp.arange(kept, dtype=jnp.int32) - kept // 2
    phase = positions[:, None] * freqs[None, :] % length
    phases = phase.astype(jnp.float32) * (2.0 * math.pi / length)
    factor = 1.0 / math.sqrt(length)
    return (jnp.cos(phases) * factor, jnp.sin(phases) * factor)


def first_table(length, kept):
    cosine, sine = fourier_parts(length, kept)
    return jnp.stack([cosine, -sine], axis=2).astype(jnp.bfloat16)


def mixing_table(length, kept):
    cosine, sine = fourier_parts(length, kept)
    real_rows = jnp.stack([cosine, sine], axis=-1)
    imag_rows = jnp.stack([-sine, cosine], axis=-1)
    return jnp.stack([real_rows, imag_rows], axis=2).astype(jnp.bfloat16)


def per_device(valence, conduction, screened, blocks, gsphere):
    held_blocks = valence.shape[0] // BLK
    cond_count = conduction.shape[0]
    slab_planes = conduction.shape[1]
    z_table = first_table(GRID_N, KF)
    mixing = mixing_table(GRID_N, KF)
    first_block = blocks[0]
    second_block = blocks[1]
    piece_first = lax.dynamic_slice_in_dim(valence, first_block % held_blocks * BLK, BLK, 0)
    piece_second = lax.dynamic_slice_in_dim(valence, second_block % held_blocks * BLK, BLK, 0)
    block_first = from_root(piece_first, BAND, first_block // held_blocks)
    block_second = broadcast(piece_second, BAND, second_block // held_blocks)
    cond_rows = jnp.transpose(conduction, (1, 2, 0))
    pair_count = BLK * cond_count
    orbitals = jnp.concatenate([block_first, block_second], axis=0)
    group_size = math.gcd(orbitals.shape[0], max(1, 128 // cond_count))
    orbital_rows = jnp.transpose(orbitals, (1, 2, 0))
    density = orbital_rows[:, :, :, None] * cond_rows[:, :, None, :]
    density = density.reshape(slab_planes, GRID_N, GRID_N, group_size * cond_count)
    z_section = jnp.einsum(
        "xyzp,zqi->xyqip", density, z_table, preferred_element_type=jnp.float32
    ).astype(jnp.bfloat16)
    y_section = jnp.einsum(
        "xyqip,ykoi->xkqop", z_section, mixing, preferred_element_type=jnp.float32
    ).astype(jnp.bfloat16)
    moved = lax.all_to_all(y_section, "grid", split_axis=1, concat_axis=0, tiled=True)
    x_section = jnp.einsum(
        "xjqip,xkoi->kjqop", moved, mixing, preferred_element_type=jnp.float32
    ).astype(jnp.bfloat16)
    flat = x_section.reshape(-1, 2, x_section.shape[-1])
    sphere = jnp.take(flat, gsphere, axis=0)
    side_first = sphere[:, :, :pair_count]
    side_second = sphere[:, :, pair_count:]
    local_rows = side_second.shape[0]
    part_rows = lax.all_gather(side_second, "grid", axis=0, tiled=True)
    flat_part = part_rows.reshape(part_rows.shape[0], 2 * pair_count)
    screened_second = jnp.dot(screened, flat_part, preferred_element_type=jnp.float32)
    screened_second = screened_second.astype(jnp.bfloat16).reshape(local_rows, 2, pair_count)
    partial_value = jnp.einsum(
        "npi,npj->ij", side_first, screened_second, preferred_element_type=jnp.float32
    )
    kernel_part = summed_on_arrival(partial_value, "grid", 0)
    return kernel_part[None]


def solution(mesh):
    split = Mesh(mesh.devices.reshape(4, 4, mesh.shape["grid"]), ("band_0", "band_1", "grid"))
    in_specs = (P(BAND, "grid", None), P(BAND, "grid", None), P("grid", None), P(), P("grid"))
    out_specs = P(BAND, "grid", None)
    return jax.shard_map(
        per_device, mesh=split, in_specs=in_specs, out_specs=out_specs, check_vma=False
    )
```

profile of v0, /device:TPU:1, one launch (start us, length us, event | category | flops | bytes accessed | tf_op | source)
XLA Modules:
  0.0 387.4 jit_solution(16740214180605855404)
XLA Ops:
  7.4 0.0 copy-start
  7.4 0.0 copy-start.1
  7.4 0.0 all-reduce.3.cloned.1.call-start
  7.4 1.4 fusion.41
  13.1 2.2 dynamic-slice_select_fusion
  15.3 0.0 all-reduce.3.cloned.1.call-update
  15.4 0.0 all-gather.6.cloned.1.call-start
  15.4 0.5 all-gather.6.cloned.1.call-update
  15.9 0.0 all-reduce.5.cloned.1.call-start
  16.6 0.2 fusion.37
  16.8 123.9 %all-reduce.3.cloned.1.call-done = bf16[8,3,9216]{2,0,1:T(8,128)(2,1)} async-done(((bf16[8,3,9216]{2,0,1:T(8,128)(2,1)}), bf16[8,3,9216]{2,0,1:T(8,128)(2,1)}) %all-reduce.3.cloned.1.call-update) | async-done | bytes 442384 | tf_op jit(solution)/shard_map/psum | solution.py:18
  140.7 0.0 all-reduce.5.cloned.1.call-update
  140.7 0.0 all-gather.6.cloned.1.call-done
  140.7 1.0 dynamic-slice_bitcast_fusion
  141.8 51.7 %all-reduce.5.cloned.1.call-done = bf16[8,3,9216]{2,0,1:T(8,128)(2,1)} async-done(((bf16[8,3,9216]{2,0,1:T(8,128)(2,1)}), bf16[8,3,9216]{2,0,1:T(8,128)(2,1)}) %all-reduce.5.cloned.1.call-update) | async-done | bytes 442384 | tf_op jit(solution)/shard_map/psum | solution.py:18
  193.5 1.1 maximum_bitcast_fusion
  194.6 0.0 copy-done.1
  194.6 3.8 broadcast_multiply_fusion
  198.4 14.4 %mul.166 = bf16[3,96,96,128]{2,1,3,0:T(8,128)(2,1)} reshape(bf16[3,9216,16,8]{1,3,2,0:T(8,128)(2,1)} %broadcast_multiply_fusion) | data formatting | bytes 14155776 | tf_op jit(solution)/shard_map/mul | solution.py:76
  212.9 12.1 %copy.26 = bf16[3,96,96,128]{3,2,1,0:T(8,128)(2,1)} copy(bf16[3,96,96,128]{2,1,3,0:T(8,128)(2,1)} %mul.166) | data formatting | bytes 14155776 | tf_op jit(solution)/shard_map/mul | solution.py:76
  225.0 4.4 %convert_bitcast_fusion = bf16[3,96,32,2,128]{4,2,1,0,3:T(8,128)(2,1)S(1)} fusion(bf16[3,96,96,128]{3,2,1,0:T(8,128)(2,1)} %copy.26, bf16[96,32,1]{0,1,2:T(8,128)(2,1)S(1)} %get-tuple-element.13, bf16[96,32,1]{0,1,2:T(8,128)(2,1)S(1)} %get-tuple-element.12), kind=kOutput, calls=%fused_computation.6 | convolution fusion | flops 455368704 | bytes 11808768 | tf_op jit(solution)/shard_map/xyzp,zqi->xyqip/dot_general | solution.py:78
  229.4 1.8 fusion.12
  231.2 1.8 copy.28
  233.0 10.9 %all-to-all-start = ((bf16[3,32,32,2,128]{4,2,0,3,1:T(8,128)(2,1)}), bf16[3,32,32,2,128]{4,2,0,3,1:T(8,128)(2,1)}, u32[]{:S(2)}, u32[]{:S(2)}) async-start(bf16[3,32,32,2,128]{4,2,0,3,1:T(8,128)(2,1)} %copy.28), calls=%async_computation | async-start | bytes 3145728 | tf_op jit(solution)/shard_map/all_to_all | solution.py:84
  243.9 0.0 all-gather.4.cloned.1.call-start
  243.9 0.0 copy-done.2
  244.0 38.2 %all-to-all-done = bf16[3,32,32,2,128]{4,2,0,3,1:T(8,128)(2,1)} async-done(((bf16[3,32,32,2,128]{4,2,0,3,1:T(8,128)(2,1)}), bf16[3,32,32,2,128]{4,2,0,3,1:T(8,128)(2,1)}, u32[]{:S(2)}, u32[]{:S(2)}) %all-to-all-start) | async-done | bytes 1572896 | tf_op jit(solution)/shard_map/all_to_all | solution.py:84
  282.2 1.8 copy.29
  284.0 1.1 fusion.21
  285.0 0.2 copy.31
  285.3 0.5 copy.32
  285.8 0.8 gather_fusion
  286.6 0.3 broadcast_select_fusion
  286.9 0.8 slice_bitcast_fusion
  287.7 0.0 all-gather.4.cloned.1.call-update
  287.8 0.1 copy.33
  287.9 66.1 %all-gather.4.cloned.1.call-done = bf16[6144,2,64]{2,1,0:T(2,128)(2,1)} async-done(((bf16[192,2,64]{2,1,0:T(2,128)(2,1)}), bf16[6144,2,64]{2,1,0:T(2,128)(2,1)}) %all-gather.4.cloned.1.call-update) | async-done | bytes 1572880 | tf_op jit(solution)/shard_map/all_gather | solution.py:93
  353.9 7.4 %copy.34 = bf16[6144,2,64]{0,2,1:T(8,128)(2,1)} copy(bf16[6144,2,64]{2,1,0:T(2,128)(2,1)} %all-gather.4.cloned.1.call-done) | data formatting | bytes 3145728 | tf_op jit(solution)/shard_map/all_gather | solution.py:93
  361.3 0.0 copy-done
  361.3 2.2 fusion.24
  363.5 0.1 copy.35
  363.6 0.2 convolution_bitcast_fusion
  363.8 0.1 reshape.170
  363.9 14.5 %all_to_all.20 = f32[32,1,128]{2,1,0:T(1,128)S(1)} all-to-all(f32[32,1,128]{2,1,0:T(1,128)S(1)} %reshape.170), channel_id=1, replica_groups=mesh['band_0'=4,'band_1'=4,'grid'=32] {'grid'}, dimensions={0} | all-to-all | bytes 32768 | tf_op jit(solution)/shard_map/all_to_all | solution.py:34
  378.4 0.5 broadcast.183
  378.9 0.7 reduce
  379.6 0.1 reshape.171
  379.7 0.6 reduce_sum.9
  (7 shorter events, 0.1 us)
Async XLA Ops:
  7.4 354.0 %copy-start = (bf16[192,6144]{1,0:T(8,128)(2,1)S(1)}, bf16[192,6144]{1,0:T(8,128)(2,1)}, u32[]{:S(2)}) copy-start(bf16[192,6144]{1,0:T(8,128)(2,1)} %param.7) | copy-start | bytes 7077892
  7.4 187.2 %copy-start.1 = (bf16[8,3,9216]{2,0,1:T(8,128)(2,1)S(1)}, bf16[8,3,9216]{2,0,1:T(8,128)(2,1)}, u32[]{:S(2)}) copy-start(bf16[8,3,9216]{2,0,1:T(8,128)(2,1)} %param.6) | copy-start | bytes 1327108
  7.4 133.3 %all-reduce.3.cloned.1.call-start = ((), (), s32[]{:S(2)}) async-start(), calls=%async_computation.2 | async-start | bytes 884736 | tf_op jit(solution)/shard_map/psum | solution.py:18
  15.4 125.4 %all-gather.6.cloned.1.call-start = ((), (), s32[]{:S(2)}) async-start(), calls=%async_computation.5 | async-start | bytes 7520256 | tf_op jit(solution)/shard_map/all_gather | solution.py:23
  15.9 177.6 %all-reduce.5.cloned.1.call-start = ((), (), s32[]{:S(2)}) async-start(), calls=%async_computation.3 | async-start | bytes 884736 | tf_op jit(solution)/shard_map/psum | solution.py:18
  231.2 12.7 %copy-start.2 = (s32[192]{0:T(256)S(1)}, s32[192]{0:T(256)}, u32[]{:S(2)}) copy-start(s32[192]{0:T(256)} %param.9) | copy-start | bytes 2308
  233.0 49.2 %all-to-all-start = ((bf16[3,32,32,2,128]{4,2,0,3,1:T(8,128)(2,1)}), bf16[3,32,32,2,128]{4,2,0,3,1:T(8,128)(2,1)}, u32[]{:S(2)}, u32[]{:S(2)}) async-start(bf16[3,32,32,2,128]{4,2,0,3,1:T(8,128)(2,1)} %copy.28), calls=%async_computation | async-start | bytes 3145728 | tf_op jit(solution)/shard_map/all_to_all | solution.py:84
  243.9 110.1 %all-gather.4.cloned.1.call-start = ((), (), s32[]{:S(2)}) async-start(), calls=%async_computation.4 | async-start | bytes 3244032 | tf_op jit(solution)/shard_map/all_gather | solution.py:93
Sparse Core Ops, SparseCore 0:
  15.5 125.1 all-reduce.2
  143.0 50.4 all-reduce.4
  287.9 66.0 all-gather.3
Sparse Core Ops, SparseCore 1:
  18.9 121.7 all-gather.5
where the time goes:
time: 389 us; the launch traced here: 387 us
  waiting for transfers between devices  281 us (72%)
  local copies, waits for them, and re-layouts  43.3 us (11%)
  between operations  19.7 us (5%)
  blocking collectives  14.5 us (4%)
  starting transfers between devices  11 us (3%)
  matrix products  9.59 us (2%)
  other arithmetic  8.83 us (2%)
    psum x2, waiting for transfers between devices, from_root(): x = lax.psum(x, axis)  176 us
    all_gather x1, waiting for transfers between devices, per_device(): part_rows = lax.all_gather(side_second, 'grid', axis=0, tiled=True)  66.1 us
    all_to_all x1, waiting for transfers between devices, per_device(): lax.all_to_all(y_section, 'grid', split_axis=1, concat_axis=0, tiled=True)  38.2 us
    mul x2, local copies, waits for them, and re-layouts, per_device(): density = orbital_rows[:, :, :, None] * cond_rows[:, :, None, :]  26.6 us
    all_to_all x1, blocking collectives, summed_on_arrival(): lax.all_to_all(blocks, axis, split_axis=0, concat_axis=0, tiled=True)  14.5 us
    all_to_all x1, starting transfers between devices, per_device(): lax.all_to_all(y_section, 'grid', split_axis=1, concat_axis=0, tiled=True)  10.9 us
  transfers between devices with their start and end apart: 5, of which 4 were waited for; matrix products, arithmetic and copies ran while one was open for 0% of the time, Pallas kernels for 0%

commit v1 on v0

v1 whole, which is shorter than its diff:
```python
import functools
import math

import jax
import jax.numpy as jnp
import ml_dtypes
import numpy as np
from jax import lax
from jax.experimental import pallas as pl
from jax.experimental.pallas import tpu as pltpu
from jax.sharding import PartitionSpec as P

GRID_N = 96
KF = 32
BLK = 8
PAIRS = 64
SIDE = 4
LANES = GRID_N * GRID_N
PART = LANES // 2
PIECE = PART // SIDE
ROWS_Y = 4
CHUNK = ROWS_Y * GRID_N
MESH = pl.DeviceIdType.MESH


def fourier_parts(length, kept):
    positions = np.arange(length)
    freqs = np.arange(kept) - kept // 2
    phases = (positions[:, None] * freqs[None, :] % length) * (2.0 * math.pi / length)
    factor = 1.0 / math.sqrt(length)
    return np.cos(phases) * factor, np.sin(phases) * factor


def first_table():
    cosine, sine = fourier_parts(GRID_N, KF)
    return np.stack([cosine, -sine], axis=2)


def mixing_table():
    cosine, sine = fourier_parts(GRID_N, KF)
    real_rows = np.stack([cosine, sine], axis=-1)
    imag_rows = np.stack([-sine, cosine], axis=-1)
    return np.stack([real_rows, imag_rows], axis=2)


def z_matrix():
    table = first_table()
    out = np.zeros((KF, ROWS_Y, 2, ROWS_Y, GRID_N))
    for y in range(ROWS_Y):
        out[:, y, :, y, :] = np.transpose(table, (1, 2, 0))
    return out.reshape(KF * ROWS_Y * 2, CHUNK).astype(ml_dtypes.bfloat16)


def mix_matrix():
    table = np.transpose(mixing_table(), (1, 2, 0, 3))
    return table.reshape(2 * KF, 2 * GRID_N).astype(ml_dtypes.bfloat16)


def remote(src, dst, send, recv, peer):
    return pltpu.make_async_remote_copy(
        src_ref=src, dst_ref=dst, send_sem=send, recv_sem=recv, device_id=peer, device_id_type=MESH
    )


def greet(peers):
    barrier = pltpu.get_barrier_semaphore()
    for peer in peers:
        pl.semaphore_signal(barrier, inc=1, device_id=peer, device_id_type=MESH)
    pl.semaphore_wait(barrier, len(peers))


def spread_kernel(
    owner_ref, src, out_ref, near0, near1, near2, near3, held, far, mine, full,
    send1, recv1, own1, send2, recv2, send3, recv3, send4, recv4,
):
    band = lax.axis_index("band")
    z, x = band // SIDE, band % SIDE
    near = (near0, near1, near2, near3)

    def along_x(k):
        return {"band": z * SIDE + (x + k) % SIDE}

    def along_z(k):
        return {"band": (z + k) % SIDE * SIDE + x}

    def lanes(q, s):
        return pl.ds(pl.multiple_of(q % 2 * PART + s * PIECE, 128), PIECE)

    greet([along_x(k) for k in (1, 2, 3)] + [along_z(k) for k in (1, 2, 3)])
    order = (2, 1, 3, 0)
    first = {}
    for j in order:
        s = (z + j) % SIDE
        for k in (2, 1, 3):
            q = (x + k) % SIDE
            copy = remote(
                src.at[q // 2, :, :, lanes(q, s)], near[j].at[x],
                send1.at[j, k - 1], recv1.at[j, k - 1], along_x(k),
            )
            copy.start()
            first[j, k] = copy
        copy = pltpu.make_async_copy(src.at[x // 2, :, :, lanes(x, s)], near[j].at[x], own1.at[j])
        copy.start()
        first[j, 0] = copy
    owner = owner_ref[x // 2]
    owner_z, owner_x = owner // SIDE, owner % SIDE
    second = []
    for j in order:
        for k in range(SIDE):
            first[j, k].wait()
        if j == 0:
            far[z] = near[j][owner_x]
        else:
            held[j] = near[j][owner_x]
            copy = remote(
                held.at[j], far.at[z], send2.at[j - 1], recv2.at[j - 1], along_z(j)
            )
            copy.start()
            second.append(copy)
    for copy in second:
        copy.wait()
    picked = far[owner_z]
    mine[...] = picked
    full[x // 2, :, :, lanes(x, z)] = picked
    third = {}
    for k in (2, 1, 3):
        copy = remote(
            mine, full.at[x // 2, :, :, lanes(x, z)], send3.at[k - 1], recv3.at[k - 1], along_z(k)
        )
        copy.start()
        third[k] = copy
    fourth = []
    for j in (0, 1, 3, 2):
        if j:
            third[j].wait()
        s = (z + SIDE - j) % SIDE
        part = full.at[x // 2, :, :, lanes(x, s)]
        for k in (2, 1, 3):
            copy = remote(
                mine if j == 0 else part, part, send4.at[j, k - 1], recv4.at[j, k - 1], along_x(k)
            )
            copy.start()
            fourth.append(copy)
    for copy in fourth:
        copy.wait()
    out_ref[...] = full[...]


def spread(owner, pieces):
    piece = (3, BLK, PIECE)
    dma = pltpu.SemaphoreType.DMA
    vmem = pl.BlockSpec(memory_space=pltpu.VMEM)
    return pl.pallas_call(
        spread_kernel,
        out_shape=jax.ShapeDtypeStruct(pieces.shape, pieces.dtype),
        in_specs=[pl.BlockSpec(memory_space=pltpu.SMEM), vmem],
        out_specs=vmem,
        scratch_shapes=[
            *[pltpu.VMEM((SIDE, *piece), jnp.bfloat16) for _ in range(SIDE)],
            pltpu.VMEM((SIDE, *piece), jnp.bfloat16),
            pltpu.VMEM((SIDE, *piece), jnp.bfloat16),
            pltpu.VMEM(piece, jnp.bfloat16),
            pltpu.VMEM(pieces.shape, jnp.bfloat16),
            dma((SIDE, 3)), dma((SIDE, 3)), dma((SIDE,)),
            dma((3,)), dma((3,)), dma((3,)), dma((3,)),
            dma((SIDE, 3)), dma((SIDE, 3)),
        ],
        compiler_params=pltpu.CompilerParams(collective_id=0, has_side_effects=True),
        name="spread_blocks",
    )(owner, pieces)


def density_kernel(chosen, cond, z_mat, mix, out_ref, sections):
    def step(j, carry):
        both = []
        for half in range(2):
            at = pl.ds(pl.multiple_of((2 * j + half) * CHUNK, 128), CHUNK)
            c = cond[0, :, at].astype(jnp.float32)
            v = jnp.concatenate(
                [chosen[0, 0, :, at].astype(jnp.float32), chosen[1, 0, :, at].astype(jnp.float32)]
            )
            dens = (v[:, None, :] * c[None, :, :]).reshape(2 * PAIRS, CHUNK).astype(jnp.bfloat16)
            part = lax.dot_general(
                z_mat[...], dens, (((1,), (1,)), ((), ())), preferred_element_type=jnp.float32
            )
            both.append(part.reshape(KF, 2 * ROWS_Y, 2 * PAIRS))
        joined = jnp.concatenate(both, axis=1).astype(jnp.bfloat16)
        sections[:, pl.ds(pl.multiple_of(j * 4 * ROWS_Y, 16), 4 * ROWS_Y), :] = joined
        return carry

    lax.fori_loop(0, LANES // CHUNK // 2, step, 0)
    for q in range(KF):
        out_ref[0, q] = jnp.dot(
            mix[...], sections[q], preferred_element_type=jnp.float32
        ).astype(jnp.bfloat16)


def densities(chosen, cond, z_mat, mix):
    planes = cond.shape[0]
    return pl.pallas_call(
        density_kernel,
        grid=(planes,),
        out_shape=jax.ShapeDtypeStruct((planes, KF, 2 * KF, 2 * PAIRS), jnp.bfloat16),
        in_specs=[
            pl.BlockSpec((2, 1, BLK, LANES), lambda i: (0, i, 0, 0)),
            pl.BlockSpec((1, BLK, LANES), lambda i: (i, 0, 0)),
            pl.BlockSpec(z_mat.shape, lambda i: (0, 0)),
            pl.BlockSpec(mix.shape, lambda i: (0, 0)),
        ],
        out_specs=pl.BlockSpec((1, KF, 2 * KF, 2 * PAIRS), lambda i: (i, 0, 0, 0)),
        scratch_shapes=[pltpu.VMEM((KF, 2 * GRID_N, 2 * PAIRS), jnp.bfloat16)],
        name="pair_density",
    )(chosen, cond, z_mat, mix)


def tail_kernel(
    devices, side_a, side_b, screened, out_ref, rows, parts, arrived,
    send, recv, own, sum_send, sum_recv,
):
    me = lax.axis_index("grid")
    half = devices // 2
    ring = half // 2
    z, y, c = me // half, me % half // 2, me % 2

    def at(zz, yy, cc):
        return zz * half + yy % ring * 2 + cc

    greet([{"grid": (me + k) % devices} for k in range(1, devices)])
    local = pltpu.make_async_copy(side_b, rows.at[me], own.at[0])
    local.start()
    started = []

    def push(slot, peer, from_input=False):
        copy = remote(
            side_b if from_input else rows.at[slot], rows.at[slot],
            send.at[len(started)], recv.at[slot], {"grid": peer},
        )
        copy.start()
        started.append(copy)

    def landed(slot):
        pltpu.make_async_remote_copy(
            src_ref=rows.at[slot], dst_ref=rows.at[slot], send_sem=own.at[0],
            recv_sem=recv.at[slot], device_id={"grid": at(z, y, 1 - c)}, device_id_type=MESH,
        ).wait_recv()

    up, down, twin = at(z, y + 1, c), at(z, y + ring - 1, c), at(z, y, 1 - c)
    push(me, at(1 - z, y, c), True)
    push(me, up, True)
    push(me, down, True)
    push(me, twin, True)
    other = at(1 - z, y, c)
    landed(other)
    push(other, up)
    push(other, down)
    push(other, twin)
    for t in range(1, ring // 2 + 1):
        for zz, ups in ((z, ring // 2), (1 - z, ring // 2 - 1)):
            for steps, back, peer in ((ups, ring - t, up), (ring - 1 - ups, t, down)):
                if t <= steps:
                    slot = at(zz, y + back, c)
                    landed(slot)
                    if t < steps:
                        push(slot, peer)
                    push(slot, twin)
    for zz in (z, 1 - z):
        for t in range(ring):
            landed(at(zz, y + t, 1 - c))
    local.wait()

    count = side_b.shape[0]

    def step(k, total):
        block = screened[:, pl.ds(pl.multiple_of(k * 2 * count, 128), 2 * count)]
        pair = rows[pl.ds(2 * k, 2)].reshape(2 * count, 2 * PAIRS)
        return total + jnp.dot(block, pair, preferred_element_type=jnp.float32)

    total = lax.fori_loop(0, half, step, jnp.zeros((count, 2 * PAIRS), jnp.float32))
    total = total.astype(jnp.bfloat16)
    product = lax.dot_general(
        side_a[...], total, (((0,), (0,)), ((), ())), preferred_element_type=jnp.float32
    )
    value = product[:PAIRS, :PAIRS] + product[PAIRS:, PAIRS:]
    width = PAIRS // devices
    for g in range(devices):
        parts[g] = value[g * width : (g + 1) * width]
    for copy in started:
        copy.wait_send()
    moves = []
    for k in range(1, devices):
        peer = (me + k) % devices
        copy = remote(
            parts.at[peer], arrived.at[k], sum_send.at[k], sum_recv.at[k], {"grid": peer}
        )
        copy.start()
        moves.append(copy)
    result = parts[me]
    for copy in moves:
        copy.wait()
    for k in range(1, devices):
        result = result + arrived[k]
    out_ref[...] = result


def tail(side_a, side_b, screened, devices):
    vmem = pl.BlockSpec(memory_space=pltpu.VMEM)
    dma = pltpu.SemaphoreType.DMA
    width = PAIRS // devices
    return pl.pallas_call(
        functools.partial(tail_kernel, devices),
        out_shape=jax.ShapeDtypeStruct((width, PAIRS), jnp.float32),
        in_specs=[vmem] * 3,
        out_specs=vmem,
        scratch_shapes=[
            pltpu.VMEM((devices, *side_b.shape), jnp.bfloat16),
            pltpu.VMEM((devices, width, PAIRS), jnp.float32),
            pltpu.VMEM((devices, width, PAIRS), jnp.float32),
            dma((devices,)), dma((devices,)), dma((1,)), dma((devices,)), dma((devices,)),
        ],
        compiler_params=pltpu.CompilerParams(collective_id=1, has_side_effects=True),
        name="screen_and_sum",
    )(side_a, side_b, screened)


def per_device(devices, valence, conduction, screened, blocks, gsphere):
    held_blocks = valence.shape[0] // BLK
    planes = conduction.shape[1]
    mix = jnp.asarray(mix_matrix())
    z_mat = jnp.asarray(z_matrix())
    by_plane = jnp.transpose(valence, (1, 0, 2))
    pieces = jnp.stack([
        lax.dynamic_slice_in_dim(by_plane, blocks[b] % held_blocks * BLK, BLK, 1) for b in range(2)
    ])
    chosen = spread(blocks // held_blocks, pieces)
    y_section = densities(chosen, jnp.transpose(conduction, (1, 0, 2)), z_mat, mix)
    blocks_y = y_section.reshape(planes, KF, KF, 2, 2 * PAIRS).transpose(2, 0, 3, 1, 4)
    moved = lax.all_to_all(blocks_y, "grid", split_axis=0, concat_axis=0, tiled=True)
    moved = moved.reshape(2 * GRID_N, KF, 2 * PAIRS)
    x_section = jnp.einsum(
        "kn,nqp->kqp", mix, moved, preferred_element_type=jnp.float32
    ).astype(jnp.bfloat16)
    flat = x_section.reshape(KF, 2, KF, 2 * PAIRS).transpose(0, 2, 1, 3).reshape(KF * KF, 2, 2 * PAIRS)
    sphere = jnp.take(flat, gsphere, axis=0)
    side_a = sphere[:, :, :PAIRS].reshape(-1, 2 * PAIRS)
    side_b = sphere[:, :, PAIRS:].reshape(-1, 2 * PAIRS)
    return tail(side_a, side_b, screened, devices)[None]


def solution(mesh):
    in_specs = (P("band", "grid", None), P("band", "grid", None), P("grid", None), P(), P("grid"))
    return jax.shard_map(
        functools.partial(per_device, mesh.shape["grid"]), mesh=mesh, in_specs=in_specs,
        out_specs=P("band", "grid", None), check_vma=False,
    )
```

time: 389 us -> 158 us (0.41)
  waiting for transfers between devices: 281 us -> 38.2 us
  Pallas kernels: 0 us -> 86.2 us
  local copies, waits for them, and re-layouts: 43.3 us -> 13.4 us
  between operations: 19.7 us -> 4.18 us
  blocking collectives: 14.5 us -> 0 us
  matrix products: 9.59 us -> 0.41 us
  other arithmetic: 8.83 us -> 2.46 us
    psum x2 -> x0, waiting for transfers between devices: 176 us -> none  [from_root(): x = lax.psum(x, axis)]
    pallas_call x0 -> x3, Pallas kernels: none -> 86.2 us  [the longest x1 37.1 us: spread(): pl.pallas_call(spread_kernel, out_shape=jax.ShapeDtypeStruct(pieces.shape...]
    all_gather x2 -> x0, waiting for transfers between devices: 66.1 us -> none  [the longest x1 66.1 us: per_device(): part_rows = lax.all_gather(side_second, 'grid', axis=0, tiled=True)]
    mul x2 -> x0, local copies, waits for them, and re-layouts: 26.6 us -> none  [per_device(): density = orbital_rows[:, :, :, None] * cond_rows[:, :, None, :]]
    all_to_all x1 -> x0, blocking collectives: 14.5 us -> none  [summed_on_arrival(): lax.all_to_all(blocks, axis, split_axis=0, concat_axis=0, tiled=True)]
    dot_general x5 -> x1, matrix products: 9.59 us -> 0.41 us  [per_device(): jnp.einsum('kn,nqp->kqp', mix, moved, preferred_element_type=jnp.float32)]
    all_gather x1 -> x0, local copies, waits for them, and re-layouts: 7.4 us -> none  [per_device(): part_rows = lax.all_gather(side_second, 'grid', axis=0, tiled=True)]
    reshape x1 -> x5, local copies, waits for them, and re-layouts: 0.54 us -> 6.66 us  [the longest x1 4.34 us: per_device(): y_section.reshape(planes, KF, KF, 2, 2 * PAIRS).transpose(2, 0, 3, 1, 4)]
  transfers between devices with their start and end apart: 5 -> 1, of which waited for: 4 -> 1; matrix products, arithmetic and copies ran while one was open for 0% -> 0% of each run, Pallas kernels for 0% -> 0%
where the time goes in v1:
time: 158 us
  Pallas kernels  86.2 us (55%)
  waiting for transfers between devices  38.2 us (24%)
  local copies, waits for them, and re-layouts  13.4 us (8%)
  starting transfers between devices  12.8 us (8%)
  between operations  4.18 us (3%)
  other arithmetic  2.46 us (2%)
    all_to_all x1, waiting for transfers between devices, per_device(): lax.all_to_all(blocks_y, 'grid', split_axis=0, concat_axis=0, tiled=True)  38.2 us
    pallas_call x1, Pallas kernels, spread(): pl.pallas_call(spread_kernel, out_shape=jax.ShapeDtypeStruct(pieces.shape...  37.1 us
    pallas_call x1, Pallas kernels, tail(): pl.pallas_call(functools.partial(tail_kernel, devices), out_shape=jax.Sha...  34.9 us
    pallas_call x1, Pallas kernels, densities(): pl.pallas_call(density_kernel, grid=(planes,), out_shape=jax.ShapeDtypeSt...  14.1 us
    all_to_all x1, starting transfers between devices, per_device(): lax.all_to_all(blocks_y, 'grid', split_axis=0, concat_axis=0, tiled=True)  12.8 us
    reshape x1, local copies, waits for them, and re-layouts, per_device(): y_section.reshape(planes, KF, KF, 2, 2 * PAIRS).transpose(2, 0, 3, 1, 4)  4.34 us
  transfers between devices with their start and end apart: 1, of which 1 were waited for; matrix products, arithmetic and copies ran while one was open for 0% of the time, Pallas kernels for 0%

profile of v1, /device:TPU:1, one launch (start us, length us, event | category | flops | bytes accessed | tf_op | source)
XLA Modules:
  0.0 157.6 jit_solution(10976772074625213173)
XLA Ops:
  0.0 1.4 fusion.1
  5.4 1.2 and_select_fusion.owner_ref
  6.6 1.3 dynamic-slice_bitcast_fusion.1
  7.9 1.0 pad_maximum_fusion.src
  8.9 37.1 %spread_blocks.1.chosen = bf16[2,3,8,9216]{3,2,1,0:T(8,128)(2,1)} custom-call(s32[2]{0:T(128)} %and_select_fusion.owner_ref, bf16[2,3,8,9216]{3,2,1,0:T(8,128)(2,1)} %pad_maximum_fusion.src), custom_call_target="tpu_custom_call" | custom-call | tf_op jit(solution)/shard_map/spread_blocks/pallas_call | solution.py:153
  46.0 14.1 %pair_density.1 = bf16[3,32,64,128]{3,2,1,0:T(8,128)(2,1)} custom-call(bf16[2,3,8,9216]{3,2,1,0:T(8,128)(2,1)} %spread_blocks.1.chosen, bf16[3,8,9216]{2,1,0:T(8,128)(2,1)} %bitcast.32, bf16[256,384]{1,0:T(8,128)(2,1)} %constant.53.clone.z_mat, bf16[64,192]{1,0:T(8,128)(2,1)} %constant.52.clone.mix), custom_call_target="tpu_custom_call" | custom-call | tf_op jit(solution)/shard_map/pair_density/pallas_call | solution.py:200
  60.1 4.3 %copy.31 = bf16[3,32,32,2,128]{4,3,1,0,2:T(2,128)(2,1)} copy(bf16[3,32,32,2,128]{4,3,2,1,0:T(2,128)(2,1)} %bitcast.28) | data formatting | bytes 3145728 | tf_op jit(solution)/shard_map/reshape | solution.py:336
  64.4 0.0 copy-start.1
  64.5 12.8 %all-to-all-start = ((bf16[32,3,2,32,128]{4,2,3,1,0:T(2,128)(2,1)}), bf16[32,3,2,32,128]{4,2,3,1,0:T(2,128)(2,1)S(1)}, u32[]{:S(2)}, u32[]{:S(2)}) async-start(bf16[32,3,2,32,128]{4,2,3,1,0:T(2,128)(2,1)} %bitcast.27), calls=%async_computation | async-start | bytes 3145728 | tf_op jit(solution)/shard_map/all_to_all | solution.py:337
  77.3 0.0 copy-done.1
  77.3 0.0 copy-start
  77.4 38.2 %all-to-all-done = bf16[32,3,2,32,128]{4,2,3,1,0:T(2,128)(2,1)S(1)} async-done(((bf16[32,3,2,32,128]{4,2,3,1,0:T(2,128)(2,1)}), bf16[32,3,2,32,128]{4,2,3,1,0:T(2,128)(2,1)S(1)}, u32[]{:S(2)}, u32[]{:S(2)}) %all-to-all-start) | async-done | bytes 1572896 | tf_op jit(solution)/shard_map/all_to_all | solution.py:337
  115.5 1.6 %copy.23 = bf16[32,3,2,32,128]{4,2,1,0,3:T(2,128)(2,1)S(1)} copy(bf16[32,3,2,32,128]{4,2,3,1,0:T(2,128)(2,1)S(1)} %all-to-all-done) | data formatting | bytes 3145728 | tf_op jit(solution)/shard_map/all_to_all | solution.py:337
  117.1 0.0 copy-done
  117.2 0.4 convolution_convert_fusion
  117.6 0.3 copy.24
  117.9 0.5 copy.25
  118.5 0.8 gather_fusion
  119.3 0.3 broadcast_select_fusion
  119.6 0.2 fusion
  119.8 0.1 copy.26
  119.9 0.7 copy.28.side_a
  120.6 0.1 copy.27
  120.7 0.7 copy.29.side_b
  121.4 34.9 %screen_and_sum.1 = f32[2,64]{1,0:T(2,128)} custom-call(bf16[192,128]{1,0:T(8,128)(2,1)} %copy.28.side_a, bf16[192,128]{1,0:T(8,128)(2,1)} %copy.29.side_b, bf16[192,6144]{1,0:T(8,128)(2,1)} %screened.1), custom_call_target="tpu_custom_call" | custom-call | tf_op jit(solution)/shard_map/screen_and_sum/pallas_call | solution.py:309
  156.4 1.2 copy.33
  (3 shorter events, 0.0 us)
Async XLA Ops:
  64.4 12.8 %copy-start.1 = (s32[192]{0:T(256)S(1)}, s32[192]{0:T(256)}, u32[]{:S(2)}) copy-start(s32[192]{0:T(256)} %param.11) | copy-start | bytes 2308
  64.5 51.1 %all-to-all-start = ((bf16[32,3,2,32,128]{4,2,3,1,0:T(2,128)(2,1)}), bf16[32,3,2,32,128]{4,2,3,1,0:T(2,128)(2,1)S(1)}, u32[]{:S(2)}, u32[]{:S(2)}) async-start(bf16[32,3,2,32,128]{4,2,3,1,0:T(2,128)(2,1)} %bitcast.27), calls=%async_computation | async-start | bytes 3145728 | tf_op jit(solution)/shard_map/all_to_all | solution.py:337
  77.3 39.8 %copy-start = (bf16[64,192,1]{1,0,2:T(8,128)(2,1)S(1)}, bf16[64,192,1]{1,0,2:T(8,128)(2,1)}, u32[]{:S(2)}) copy-start(bf16[64,192,1]{1,0,2:T(8,128)(2,1)} %constant.56) | copy-start | bytes 73732

commit v2 on v1

--- a/solution.py
+++ b/solution.py
@@ -20,12 +20,15 @@
 PIECE = PART // SIDE
 ROWS_Y = 4
 CHUNK = ROWS_Y * GRID_N
+NEG = KF // 2 + 1
+FULL_X = KF + 1
+ROWS_X = 48
 MESH = pl.DeviceIdType.MESH
 
 
 def fourier_parts(length, kept):
     positions = np.arange(length)
-    freqs = np.arange(kept) - kept // 2
+    freqs = np.arange(kept) - KF // 2
     phases = (positions[:, None] * freqs[None, :] % length) * (2.0 * math.pi / length)
     factor = 1.0 / math.sqrt(length)
     return np.cos(phases) * factor, np.sin(phases) * factor
@@ -36,24 +39,32 @@
     return np.stack([cosine, -sine], axis=2)
 
 
-def mixing_table():
-    cosine, sine = fourier_parts(GRID_N, KF)
+def mixing_table(kept):
+    cosine, sine = fourier_parts(GRID_N, kept)
     real_rows = np.stack([cosine, sine], axis=-1)
     imag_rows = np.stack([-sine, cosine], axis=-1)
     return np.stack([real_rows, imag_rows], axis=2)
 
 
 def z_matrix():
-    table = first_table()
-    out = np.zeros((KF, ROWS_Y, 2, ROWS_Y, GRID_N))
+    table = first_table()[:, :NEG]
+    out = np.zeros((NEG, ROWS_Y, 2, ROWS_Y, GRID_N))
     for y in range(ROWS_Y):
         out[:, y, :, y, :] = np.transpose(table, (1, 2, 0))
-    return out.reshape(KF * ROWS_Y * 2, CHUNK).astype(ml_dtypes.bfloat16)
-
-
-def mix_matrix():
-    table = np.transpose(mixing_table(), (1, 2, 0, 3))
-    return table.reshape(2 * KF, 2 * GRID_N).astype(ml_dtypes.bfloat16)
+    return out.reshape(NEG * ROWS_Y * 2, CHUNK).astype(ml_dtypes.bfloat16)
+
+
+def y_matrix():
+    table = np.transpose(mixing_table(KF), (1, 2, 0, 3))
+    lowest = table[:1] * np.array([1.0, -1.0])
+    return np.concatenate([table, lowest]).reshape(2 * KF + 2, 2 * GRID_N).astype(ml_dtypes.bfloat16)
+
+
+def x_matrix():
+    table = np.transpose(mixing_table(FULL_X), (2, 1, 0, 3)).reshape(2, FULL_X, 2 * GRID_N)
+    out = np.zeros((2, ROWS_X, 2 * GRID_N))
+    out[:, :FULL_X] = table
+    return out.reshape(2 * ROWS_X, 2 * GRID_N).astype(ml_dtypes.bfloat16)
 
 
 def remote(src, dst, send, recv, peer):
@@ -183,13 +194,13 @@
             part = lax.dot_general(
                 z_mat[...], dens, (((1,), (1,)), ((), ())), preferred_element_type=jnp.float32
             )
-            both.append(part.reshape(KF, 2 * ROWS_Y, 2 * PAIRS))
+            both.append(part.reshape(NEG, 2 * ROWS_Y, 2 * PAIRS))
         joined = jnp.concatenate(both, axis=1).astype(jnp.bfloat16)
         sections[:, pl.ds(pl.multiple_of(j * 4 * ROWS_Y, 16), 4 * ROWS_Y), :] = joined
         return carry
 
     lax.fori_loop(0, LANES // CHUNK // 2, step, 0)
-    for q in range(KF):
+    for q in range(NEG):
         out_ref[0, q] = jnp.dot(
             mix[...], sections[q], preferred_element_type=jnp.float32
         ).astype(jnp.bfloat16)
@@ -200,22 +211,57 @@
     return pl.pallas_call(
         density_kernel,
         grid=(planes,),
-        out_shape=jax.ShapeDtypeStruct((planes, KF, 2 * KF, 2 * PAIRS), jnp.bfloat16),
+        out_shape=jax.ShapeDtypeStruct((planes, NEG, 2 * KF + 2, 2 * PAIRS), jnp.bfloat16),
         in_specs=[
             pl.BlockSpec((2, 1, BLK, LANES), lambda i: (0, i, 0, 0)),
             pl.BlockSpec((1, BLK, LANES), lambda i: (i, 0, 0)),
             pl.BlockSpec(z_mat.shape, lambda i: (0, 0)),
             pl.BlockSpec(mix.shape, lambda i: (0, 0)),
         ],
-        out_specs=pl.BlockSpec((1, KF, 2 * KF, 2 * PAIRS), lambda i: (i, 0, 0, 0)),
-        scratch_shapes=[pltpu.VMEM((KF, 2 * GRID_N, 2 * PAIRS), jnp.bfloat16)],
+        out_specs=pl.BlockSpec((1, NEG, 2 * KF + 2, 2 * PAIRS), lambda i: (i, 0, 0, 0)),
+        scratch_shapes=[pltpu.VMEM((NEG, 2 * GRID_N, 2 * PAIRS), jnp.bfloat16)],
         name="pair_density",
     )(chosen, cond, z_mat, mix)
 
 
+def one_hot(index, count):
+    lanes = lax.broadcasted_iota(jnp.int32, (index.shape[0], count), 1)
+    return jnp.where(lanes == index, 1.0, 0.0).astype(jnp.bfloat16)
+
+
+def sphere_kernel(moved, mix, own_at, twin_at, own_ref, twin_ref, table_ref, table):
+    for q in range(NEG + 1):
+        part = jnp.dot(mix[...], moved[q], preferred_element_type=jnp.float32)
+        both = jnp.concatenate([part[:ROWS_X], part[ROWS_X:]], axis=1).astype(jnp.bfloat16)
+        if q < NEG:
+            table[q * ROWS_X : (q + 1) * ROWS_X] = both
+        else:
+            table_ref[...] = both[:KF]
+    count = table.shape[0]
+    own = jnp.dot(one_hot(own_at[...], count), table[...], preferred_element_type=jnp.float32)
+    own_ref[...] = own.astype(jnp.bfloat16)
+    twin = jnp.dot(one_hot(twin_at[...], count), table[...], preferred_element_type=jnp.float32)
+    lanes = lax.broadcasted_iota(jnp.int32, twin.shape, 1)
+    twin_ref[...] = jnp.where(lanes < 2 * PAIRS, twin, -twin).astype(jnp.bfloat16)
+
+
+def spheres(moved, mix, own_at, twin_at):
+    rows = jax.ShapeDtypeStruct((own_at.shape[0], 4 * PAIRS), jnp.bfloat16)
+    vmem = pl.BlockSpec(memory_space=pltpu.VMEM)
+    return pl.pallas_call(
+        sphere_kernel,
+        out_shape=[rows, rows, jax.ShapeDtypeStruct((KF, 4 * PAIRS), jnp.bfloat16)],
+        in_specs=[vmem] * 4,
+        out_specs=[vmem] * 3,
+        scratch_shapes=[pltpu.VMEM((NEG * ROWS_X, 4 * PAIRS), jnp.bfloat16)],
+        name="x_and_sphere",
+    )(moved, mix, own_at, twin_at)
+
+
 def tail_kernel(
-    devices, side_a, side_b, screened, out_ref, rows, parts, arrived,
-    send, recv, own, sum_send, sum_recv,
+    devices, own_rows, twin_rows, table, lone_at, screened, out_ref,
+    got, tables, side_a, side_b, rows, parts, arrived,
+    swap_send, swap_recv, lone_send, lone_recv, send, recv, own, sum_send, sum_recv,
 ):
     me = lax.axis_index("grid")
     half = devices // 2
@@ -226,6 +272,50 @@
         return zz * half + yy % ring * 2 + cc
 
     greet([{"grid": (me + k) % devices} for k in range(1, devices)])
+    paired = (me != 0) & (me != half)
+    swap = remote(
+        twin_rows, got, swap_send.at[0], swap_recv.at[0], {"grid": (devices - me) % devices}
+    )
+    helper = (me > 0) & (me < half)
+
+    @pl.when(helper)
+    def _():
+        remote(
+            table, tables.at[me - 1], lone_send.at[0], lone_recv.at[me - 1], {"grid": 0}
+        ).start()
+
+    @pl.when(paired)
+    def _():
+        swap.start()
+        swap.wait()
+
+    @pl.when(me == half)
+    def _():
+        got[...] = twin_rows[...]
+
+    @pl.when(me == 0)
+    def _():
+        for i in range(half - 1):
+            remote(
+                table, tables.at[i], lone_send.at[0], lone_recv.at[i], {"grid": i + 1}
+            ).wait_recv()
+        count = (half - 1) * KF
+        picked = jnp.dot(
+            one_hot(lone_at[...], count), tables[...].reshape(count, 4 * PAIRS),
+            preferred_element_type=jnp.float32,
+        )
+        got[...] = picked.astype(jnp.bfloat16)
+
+    @pl.when(helper)
+    def _():
+        remote(
+            table, tables.at[me - 1], lone_send.at[0], lone_recv.at[me - 1], {"grid": 0}
+        ).wait_send()
+
+    sphere = own_rows[...].astype(jnp.float32) + got[...].astype(jnp.float32)
+    real, imag = sphere[:, : 2 * PAIRS], sphere[:, 2 * PAIRS :]
+    side_b[...] = jnp.concatenate([real[:, PAIRS:], imag[:, PAIRS:]], axis=1).astype(jnp.bfloat16)
+    side_a[...] = jnp.concatenate([real[:, :PAIRS], imag[:, :PAIRS]], axis=1).astype(jnp.bfloat16)
     local = pltpu.make_async_copy(side_b, rows.at[me], own.at[0])
     local.start()
     started = []
@@ -302,48 +392,59 @@
     out_ref[...] = result
 
 
-def tail(side_a, side_b, screened, devices):
+def tail(own_rows, twin_rows, table, lone_at, screened, devices):
     vmem = pl.BlockSpec(memory_space=pltpu.VMEM)
     dma = pltpu.SemaphoreType.DMA
     width = PAIRS // devices
+    side = (own_rows.shape[0], 2 * PAIRS)
     return pl.pallas_call(
         functools.partial(tail_kernel, devices),
         out_shape=jax.ShapeDtypeStruct((width, PAIRS), jnp.float32),
-        in_specs=[vmem] * 3,
+        in_specs=[vmem] * 5,
         out_specs=vmem,
         scratch_shapes=[
-            pltpu.VMEM((devices, *side_b.shape), jnp.bfloat16),
+            pltpu.VMEM(own_rows.shape, jnp.bfloat16),
+            pltpu.VMEM((devices // 2 - 1, *table.shape), jnp.bfloat16),
+            pltpu.VMEM(side, jnp.bfloat16),
+            pltpu.VMEM(side, jnp.bfloat16),
+            pltpu.VMEM((devices, *side), jnp.bfloat16),
             pltpu.VMEM((devices, width, PAIRS), jnp.float32),
             pltpu.VMEM((devices, width, PAIRS), jnp.float32),
+            dma((1,)), dma((1,)), dma((1,)), dma((devices // 2 - 1,)),
             dma((devices,)), dma((devices,)), dma((1,)), dma((devices,)), dma((devices,)),
         ],
         compiler_params=pltpu.CompilerParams(collective_id=1, has_side_effects=True),
         name="screen_and_sum",
-    )(side_a, side_b, screened)
+    )(own_rows, twin_rows, table, lone_at, screened)
 
 
 def per_device(devices, valence, conduction, screened, blocks, gsphere):
     held_blocks = valence.shape[0] // BLK
     planes = conduction.shape[1]
-    mix = jnp.asarray(mix_matrix())
-    z_mat = jnp.asarray(z_matrix())
+    twin_points = lax.ppermute(
+        gsphere, "grid", [(g, (devices - g) % devices) for g in range(devices)]
+    )
     by_plane = jnp.transpose(valence, (1, 0, 2))
     pieces = jnp.stack([
         lax.dynamic_slice_in_dim(by_plane, blocks[b] % held_blocks * BLK, BLK, 1) for b in range(2)
     ])
     chosen = spread(blocks // held_blocks, pieces)
-    y_section = densities(chosen, jnp.transpose(conduction, (1, 0, 2)), z_mat, mix)
-    blocks_y = y_section.reshape(planes, KF, KF, 2, 2 * PAIRS).transpose(2, 0, 3, 1, 4)
+    y_section = densities(
+        chosen, jnp.transpose(conduction, (1, 0, 2)), jnp.asarray(z_matrix()), jnp.asarray(y_matrix())
+    )
+    blocks_y = y_section[:, :, : 2 * KF].reshape(planes, NEG, KF, 2, 2 * PAIRS)
+    lowest = jnp.flip(y_section[:, :, 2 * KF :], axis=1)
+    lowest = jnp.pad(lowest, ((0, 0), (0, KF - NEG), (0, 0), (0, 0)))
+    blocks_y = jnp.concatenate([blocks_y, lowest[:, None]], axis=1).transpose(2, 0, 3, 1, 4)
     moved = lax.all_to_all(blocks_y, "grid", split_axis=0, concat_axis=0, tiled=True)
-    moved = moved.reshape(2 * GRID_N, KF, 2 * PAIRS)
-    x_section = jnp.einsum(
-        "kn,nqp->kqp", mix, moved, preferred_element_type=jnp.float32
-    ).astype(jnp.bfloat16)
-    flat = x_section.reshape(KF, 2, KF, 2 * PAIRS).transpose(0, 2, 1, 3).reshape(KF * KF, 2, 2 * PAIRS)
-    sphere = jnp.take(flat, gsphere, axis=0)
-    side_a = sphere[:, :, :PAIRS].reshape(-1, 2 * PAIRS)
-    side_b = sphere[:, :, PAIRS:].reshape(-1, 2 * PAIRS)
-    return tail(side_a, side_b, screened, devices)[None]
+    moved = moved.reshape(2 * GRID_N, NEG + 1, 2 * PAIRS).transpose(1, 0, 2)
+    qx, qz = gsphere // KF, gsphere % KF
+    twin_qx, twin_qz = twin_points // KF, twin_points % KF
+    own_at = jnp.where(qz < NEG, qz * ROWS_X + qx, -1)[:, None]
+    lone_at = jnp.where(qz < NEG, -1, (qz - NEG) * KF + qx)[:, None]
+    twin_at = jnp.where(twin_qz < NEG, -1, (KF - twin_qz) * ROWS_X + KF - twin_qx)[:, None]
+    own_rows, twin_rows, table = spheres(moved, jnp.asarray(x_matrix()), own_at, twin_at)
+    return tail(own_rows, twin_rows, table, lone_at, screened, devices)[None]
 
 
 def solution(mesh):

time: 158 us -> 147 us (0.930)
  waiting for transfers between devices: 38.2 us -> 15.2 us
  Pallas kernels: 86.2 us -> 96.1 us
  starting transfers between devices: 12.8 us -> 18.2 us
  local copies, waits for them, and re-layouts: 13.4 us -> 9.13 us
    all_to_all x1, waiting for transfers between devices: 38.2 us -> 1.09 us  [per_device(): lax.all_to_all(blocks_y, 'grid', split_axis=0, concat_axis=0, tiled=True)]
    ppermute x0 -> x1, waiting for transfers between devices: none -> 14.1 us  [per_device(): lax.ppermute(gsphere, 'grid', [(g, (devices - g) % devices) for g in rang...]
    pallas_call x1, Pallas kernels: 34.9 us -> 44.4 us  [tail(): pl.pallas_call(functools.partial(tail_kernel, devices), out_shape=jax.Sha...]
    reshape x5 -> x0, local copies, waits for them, and re-layouts: 6.66 us -> none  [the longest x1 4.34 us: per_device(): y_section.reshape(planes, KF, KF, 2, 2 * PAIRS).transpose(2, 0, 3, 1, 4)]
    ppermute x0 -> x1, starting transfers between devices: none -> 5.46 us  [per_device(): lax.ppermute(gsphere, 'grid', [(g, (devices - g) % devices) for g in rang...]
    pallas_call x0 -> x1, Pallas kernels: none -> 2.53 us  [spheres(): pl.pallas_call(sphere_kernel, out_shape=[rows, rows, jax.ShapeDtypeStruct...]
    broadcast_in_dim x0 -> x3, local copies, waits for them, and re-layouts: none -> 2.3 us  [the longest x1 0.77 us: per_device(): own_at = jnp.where(qz < NEG, qz * ROWS_X + qx, -1)[:, None]]
    pallas_call x1, Pallas kernels: 14.1 us -> 12 us  [densities(): pl.pallas_call(density_kernel, grid=(planes,), out_shape=jax.ShapeDtypeSt...]
  transfers between devices with their start and end apart: 1 -> 2, of which waited for: 1 -> 2; matrix products, arithmetic and copies ran while one was open for 0% -> 2% of each run, Pallas kernels for 0% -> 0%
where the time goes in v2:
time: 147 us; the launch traced here: 146 us
  Pallas kernels  96.1 us (65%)
  starting transfers between devices  18.2 us (12%)
  waiting for transfers between devices  15.2 us (10%)
  local copies, waits for them, and re-layouts  9.13 us (6%)
  other arithmetic  3.95 us (3%)
  between operations  3.93 us (3%)
    pallas_call x1, Pallas kernels, tail(): pl.pallas_call(functools.partial(tail_kernel, devices), out_shape=jax.Sha...  44.4 us
    pallas_call x1, Pallas kernels, spread(): pl.pallas_call(spread_kernel, out_shape=jax.ShapeDtypeStruct(pieces.shape...  37.2 us
    ppermute x1, waiting for transfers between devices, per_device(): lax.ppermute(gsphere, 'grid', [(g, (devices - g) % devices) for g in rang...  14.1 us
    all_to_all x1, starting transfers between devices, per_device(): lax.all_to_all(blocks_y, 'grid', split_axis=0, concat_axis=0, tiled=True)  12.7 us
    pallas_call x1, Pallas kernels, densities(): pl.pallas_call(density_kernel, grid=(planes,), out_shape=jax.ShapeDtypeSt...  12 us
    ppermute x1, starting transfers between devices, per_device(): lax.ppermute(gsphere, 'grid', [(g, (devices - g) % devices) for g in rang...  5.46 us
  transfers between devices with their start and end apart: 2, of which 2 were waited for; matrix products, arithmetic and copies ran while one was open for 2% of the time, Pallas kernels for 0%

profile of v2, /device:TPU:1, one launch (start us, length us, event | category | flops | bytes accessed | tf_op | source)
XLA Modules:
  0.0 146.5 jit_solution(6597640513137410301)
XLA Ops:
  0.0 1.4 fusion.1
  5.2 1.2 and_select_fusion.4.owner_ref
  6.4 1.3 dynamic-slice_bitcast_fusion.1
  7.7 1.0 pad_maximum_fusion.src
  8.7 37.2 %spread_blocks.1.chosen = bf16[2,3,8,9216]{3,2,1,0:T(8,128)(2,1)} custom-call(s32[2]{0:T(128)} %and_select_fusion.4.owner_ref, bf16[2,3,8,9216]{3,2,1,0:T(8,128)(2,1)} %pad_maximum_fusion.src), custom_call_target="tpu_custom_call" | custom-call | tf_op jit(solution)/shard_map/spread_blocks/pallas_call | solution.py:164
  45.9 12.0 %pair_density.1 = bf16[3,17,66,128]{3,2,1,0:T(8,128)(2,1)} custom-call(bf16[2,3,8,9216]{3,2,1,0:T(8,128)(2,1)} %spread_blocks.1.chosen, bf16[3,8,9216]{2,1,0:T(8,128)(2,1)} %bitcast.27, bf16[136,384]{1,0:T(8,128)(2,1)} %constant.86.clone.z_mat, bf16[66,192]{1,0:T(8,128)(2,1)} %constant.87.clone.mix), custom_call_target="tpu_custom_call" | custom-call | tf_op jit(solution)/shard_map/pair_density/pallas_call | solution.py:211
  57.9 0.0 slice-start
  57.9 1.0 slice.17
  58.9 0.0 copy-start
  58.9 0.2 slice-done
  59.1 1.7 %maximum_bitcast_fusion = bf16[32,3,2,18,128]{4,2,1,3,0:T(2,128)(2,1)} fusion(bf16[3,17,32,2,128]{4,3,2,1,0:T(2,128)(2,1)S(1)} %bitcast.26, bf16[3,17,2,128]{3,2,1,0:T(2,128)(2,1)S(1)} %rev.4), kind=kLoop, calls=%fused_computation.1 | loop fusion | flops 1769472 | bytes 1746432 | tf_op jit(solution)/shard_map/transpose | solution.py:438
  60.8 12.7 %all-to-all-start = ((bf16[32,3,2,18,128]{4,2,1,3,0:T(2,128)(2,1)}), bf16[32,3,2,18,128]{4,2,1,3,0:T(2,128)(2,1)S(1)}, u32[]{:S(2)}, u32[]{:S(2)}) async-start(bf16[32,3,2,18,128]{4,2,1,3,0:T(2,128)(2,1)} %maximum_bitcast_fusion), calls=%async_computation | async-start | bytes 1769472 | tf_op jit(solution)/shard_map/all_to_all | solution.py:439
  73.5 0.0 copy-done
  73.5 5.5 %collective-permute-start = (s32[192]{0:T(256)S(1)}, s32[192]{0:T(256)S(1)}, u32[]{:S(2)}, u32[]{:S(2)}) collective-permute-start(s32[192]{0:T(256)S(1)} %copy-done), channel_id=1, source_target_pairs={{0,0},{1,31},{2,30},{3,29},{4,28},{5,27},{6,26},{7,25},{8,24},{9,2... | collective-permute-start | bytes 2312 | tf_op jit(solution)/shard_map/ppermute | solution.py:424
  79.0 0.8 copy.19.own_at
  79.8 0.8 copy.21.lone_at
  80.5 14.1 %collective-permute-done = s32[192]{0:T(256)S(1)} collective-permute-done((s32[192]{0:T(256)S(1)}, s32[192]{0:T(256)S(1)}, u32[]{:S(2)}, u32[]{:S(2)}) %collective-permute-start) | collective-permute-done | bytes 800 | tf_op jit(solution)/shard_map/ppermute | solution.py:424
  94.7 0.8 copy.20.twin_at
  95.5 1.1 all-to-all-done
  96.6 1.8 %copy.18 = bf16[32,3,2,18,128]{4,2,1,0,3:T(2,128)(2,1)} copy(bf16[32,3,2,18,128]{4,2,1,3,0:T(2,128)(2,1)S(1)} %all-to-all-done) | data formatting | bytes 1769472 | tf_op jit(solution)/shard_map/all_to_all | solution.py:439
  98.3 2.5 %x_and_sphere.1 = (bf16[192,256]{1,0:T(8,128)(2,1)}, bf16[192,256]{1,0:T(8,128)(2,1)}, bf16[32,256]{1,0:T(8,128)(2,1)}) custom-call(bf16[18,192,128]{2,1,0:T(8,128)(2,1)} %bitcast.25, bf16[96,192]{1,0:T(8,128)(2,1)} %constant.88.clone.mix, s32[192,1]{1,0:T(8,128)} %copy.19.own_at, s32[192,1]{1,0:T(8,128)} %copy.20.twin_at), custom_call_target="tpu_custom_call" | custom-call | tf_op jit(solution)/shard_map/x_and_sphere/pallas_call | solution.py:251
  100.9 44.4 %screen_and_sum.1 = f32[2,64]{1,0:T(2,128)} custom-call(bf16[192,256]{1,0:T(8,128)(2,1)} %get-tuple-element.8.own_rows, bf16[192,256]{1,0:T(8,128)(2,1)} %get-tuple-element.9.twin_rows, bf16[32,256]{1,0:T(8,128)(2,1)} %get-tuple-element.10.table, s32[192,1]{1,0:T(8,128)} %copy.21.lone_at, bf16[192,6144]{1,0:T(8,128)(2,1)} %screened.1), custom_call_target="tpu_custom_call" | custom-call | tf_op jit(solution)/shard_map/screen_and_sum/pallas_call | solution.py:400
  145.3 1.2 copy.27
  (4 shorter events, 0.1 us)
Async XLA Ops:
  57.9 1.2 slice-start
  58.9 14.6 %copy-start = (s32[192]{0:T(256)S(1)}, s32[192]{0:T(256)}, u32[]{:S(2)}) copy-start(s32[192]{0:T(256)} %param.12) | copy-start | bytes 2308
  60.8 35.8 %all-to-all-start = ((bf16[32,3,2,18,128]{4,2,1,3,0:T(2,128)(2,1)}), bf16[32,3,2,18,128]{4,2,1,3,0:T(2,128)(2,1)S(1)}, u32[]{:S(2)}, u32[]{:S(2)}) async-start(bf16[32,3,2,18,128]{4,2,1,3,0:T(2,128)(2,1)} %maximum_bitcast_fusion), calls=%async_computation | async-start | bytes 1769472 | tf_op jit(solution)/shard_map/all_to_all | solution.py:439
  73.5 21.2 %collective-permute-start = (s32[192]{0:T(256)S(1)}, s32[192]{0:T(256)S(1)}, u32[]{:S(2)}, u32[]{:S(2)}) collective-permute-start(s32[192]{0:T(256)S(1)} %copy-done), channel_id=1, source_target_pairs={{0,0},{1,31},{2,30},{3,29},{4,28},{5,27},{6,26},{7,25},{8,24},{9,2... | collective-permute-start | bytes 2312 | tf_op jit(solution)/shard_map/ppermute | solution.py:424

commit v3 on v2

--- a/solution.py
+++ b/solution.py
@@ -81,7 +81,7 @@
 
 
 def spread_kernel(
-    owner_ref, src, out_ref, near0, near1, near2, near3, held, far, mine, full,
+    blocks_ref, held_bands, out_ref, src, near0, near1, near2, near3, held, far, mine, full,
     send1, recv1, own1, send2, recv2, send3, recv3, send4, recv4,
 ):
     band = lax.axis_index("band")
@@ -97,6 +97,9 @@
     def lanes(q, s):
         return pl.ds(pl.multiple_of(q % 2 * PART + s * PIECE, 128), PIECE)
 
+    count = held_bands.shape[1]
+    for b in range(2):
+        src[b] = held_bands[:, lax.rem(blocks_ref[b], count)]
     greet([along_x(k) for k in (1, 2, 3)] + [along_z(k) for k in (1, 2, 3)])
     order = (2, 1, 3, 0)
     first = {}
@@ -113,7 +116,7 @@
         copy = pltpu.make_async_copy(src.at[x // 2, :, :, lanes(x, s)], near[j].at[x], own1.at[j])
         copy.start()
         first[j, 0] = copy
-    owner = owner_ref[x // 2]
+    owner = lax.div(blocks_ref[x // 2], count)
     owner_z, owner_x = owner // SIDE, owner % SIDE
     second = []
     for j in order:
@@ -157,28 +160,31 @@
     out_ref[...] = full[...]
 
 
-def spread(owner, pieces):
-    piece = (3, BLK, PIECE)
+def spread(blocks, held_bands):
+    planes = held_bands.shape[0]
+    whole = (2, planes, BLK, LANES)
+    piece = (planes, BLK, PIECE)
     dma = pltpu.SemaphoreType.DMA
     vmem = pl.BlockSpec(memory_space=pltpu.VMEM)
     return pl.pallas_call(
         spread_kernel,
-        out_shape=jax.ShapeDtypeStruct(pieces.shape, pieces.dtype),
+        out_shape=jax.ShapeDtypeStruct(whole, jnp.bfloat16),
         in_specs=[pl.BlockSpec(memory_space=pltpu.SMEM), vmem],
         out_specs=vmem,
         scratch_shapes=[
+            pltpu.VMEM(whole, jnp.bfloat16),
             *[pltpu.VMEM((SIDE, *piece), jnp.bfloat16) for _ in range(SIDE)],
             pltpu.VMEM((SIDE, *piece), jnp.bfloat16),
             pltpu.VMEM((SIDE, *piece), jnp.bfloat16),
             pltpu.VMEM(piece, jnp.bfloat16),
-            pltpu.VMEM(pieces.shape, jnp.bfloat16),
+            pltpu.VMEM(whole, jnp.bfloat16),
             dma((SIDE, 3)), dma((SIDE, 3)), dma((SIDE,)),
             dma((3,)), dma((3,)), dma((3,)), dma((3,)),
             dma((SIDE, 3)), dma((SIDE, 3)),
         ],
         compiler_params=pltpu.CompilerParams(collective_id=0, has_side_effects=True),
         name="spread_blocks",
-    )(owner, pieces)
+    )(blocks, held_bands)
 
 
 def density_kernel(chosen, cond, z_mat, mix, out_ref, sections):
@@ -224,6 +230,51 @@
     )(chosen, cond, z_mat, mix)
 
 
+def exchange_kernel(devices, src, out_ref, kept, send, recv, own):
+    me = lax.axis_index("grid")
+    half = devices // 2
+    ring = half // 2
+    z, y, c = me // half, me % half // 2, me % 2
+    greet([{"grid": (me + k) % devices} for k in range(1, devices)])
+    inward = pltpu.make_async_copy(src.at[me], kept, own.at[0])
+    inward.start()
+    moves = []
+    for dy in sorted(range(ring), key=lambda d: -min(d, ring - d)):
+        for dz in (1, 0):
+            for dc in (0, 1):
+                k = dz * half + dy * 2 + dc
+                if k:
+                    peer = (z + dz) % 2 * half + (y + dy) % ring * 2 + (c + dc) % 2
+                    copy = remote(
+                        src.at[peer], out_ref.at[me], send.at[k], recv.at[k], {"grid": peer}
+                    )
+                    copy.start()
+                    moves.append((dy, dz, dc, k, copy))
+    inward.wait()
+    outward = pltpu.make_async_copy(kept, out_ref.at[me], own.at[1])
+    outward.start()
+    for dy, dz, dc, k, copy in moves:
+        copy.wait_send()
+        peer = (z + dz) % 2 * half + (y + ring - dy) % ring * 2 + (c + dc) % 2
+        remote(src.at[peer], out_ref.at[peer], send.at[k], recv.at[k], {"grid": peer}).wait_recv()
+    outward.wait()
+
+
+def exchange(blocks, devices):
+    dma = pltpu.SemaphoreType.DMA
+    return pl.pallas_call(
+        functools.partial(exchange_kernel, devices),
+        out_shape=jax.ShapeDtypeStruct(blocks.shape, blocks.dtype),
+        in_specs=[pl.BlockSpec(memory_space=pl.ANY)],
+        out_specs=pl.BlockSpec(memory_space=pl.ANY),
+        scratch_shapes=[
+            pltpu.VMEM(blocks.shape[1:], blocks.dtype), dma((devices,)), dma((devices,)), dma((2,))
+        ],
+        compiler_params=pltpu.CompilerParams(collective_id=2, has_side_effects=True),
+        name="planes_for_frequencies",
+    )(blocks)
+
+
 def one_hot(index, count):
     lanes = lax.broadcasted_iota(jnp.int32, (index.shape[0], count), 1)
     return jnp.where(lanes == index, 1.0, 0.0).astype(jnp.bfloat16)
@@ -260,9 +311,11 @@
 
 def tail_kernel(
     devices, own_rows, twin_rows, table, lone_at, screened, out_ref,
-    got, tables, side_a, side_b, rows, parts, arrived,
-    swap_send, swap_recv, lone_send, lone_recv, send, recv, own, sum_send, sum_recv,
+    weights, total, got, tables, side_a, side_b, rows, parts, arrived,
+    swap_send, swap_recv, lone_send, lone_recv, send, recv, own, sum_send, sum_recv, fetched,
 ):
+    fetch = pltpu.make_async_copy(screened, weights, fetched.at[0])
+    fetch.start()
     me = lax.axis_index("grid")
     half = devices // 2
     ring = half // 2
@@ -344,7 +397,21 @@
     push(other, up)
     push(other, down)
     push(other, twin)
+    count = side_a.shape[0]
+    total[...] = jnp.zeros_like(total)
+    local.wait()
+    fetch.wait()
+
+    def screen(zz, back):
+        landed(at(zz, y + back, 1 - c))
+        first = at(zz, y + back, 0)
+        columns = pl.ds(pl.multiple_of(first * count, 128), 2 * count)
+        pair = rows[pl.ds(first, 2)].reshape(2 * count, 2 * PAIRS)
+        total[...] += jnp.dot(weights[:, columns], pair, preferred_element_type=jnp.float32)
+
+    ready = [(z, 0), (1 - z, 0)]
     for t in range(1, ring // 2 + 1):
+        fresh = []
         for zz, ups in ((z, ring // 2), (1 - z, ring // 2 - 1)):
             for steps, back, peer in ((ups, ring - t, up), (ring - 1 - ups, t, down)):
                 if t <= steps:
@@ -353,22 +420,14 @@
                     if t < steps:
                         push(slot, peer)
                     push(slot, twin)
-    for zz in (z, 1 - z):
-        for t in range(ring):
-            landed(at(zz, y + t, 1 - c))
-    local.wait()
-
-    count = side_b.shape[0]
-
-    def step(k, total):
-        block = screened[:, pl.ds(pl.multiple_of(k * 2 * count, 128), 2 * count)]
-        pair = rows[pl.ds(2 * k, 2)].reshape(2 * count, 2 * PAIRS)
-        return total + jnp.dot(block, pair, preferred_element_type=jnp.float32)
-
-    total = lax.fori_loop(0, half, step, jnp.zeros((count, 2 * PAIRS), jnp.float32))
-    total = total.astype(jnp.bfloat16)
+                    fresh.append((zz, back))
+        for pair in ready:
+            screen(*pair)
+        ready = fresh
+    for pair in ready:
+        screen(*pair)
     product = lax.dot_general(
-        side_a[...], total, (((0,), (0,)), ((), ())), preferred_element_type=jnp.float32
+        side_a[...], total[...].astype(jnp.bfloat16), (((0,), (0,)), ((), ())), preferred_element_type=jnp.float32
     )
     value = product[:PAIRS, :PAIRS] + product[PAIRS:, PAIRS:]
     width = PAIRS // devices
@@ -400,9 +459,11 @@
     return pl.pallas_call(
         functools.partial(tail_kernel, devices),
         out_shape=jax.ShapeDtypeStruct((width, PAIRS), jnp.float32),
-        in_specs=[vmem] * 5,
+        in_specs=[vmem] * 4 + [pl.BlockSpec(memory_space=pl.ANY)],
         out_specs=vmem,
         scratch_shapes=[
+            pltpu.VMEM(screened.shape, jnp.bfloat16),
+            pltpu.VMEM(side, jnp.float32),
             pltpu.VMEM(own_rows.shape, jnp.bfloat16),
             pltpu.VMEM((devices // 2 - 1, *table.shape), jnp.bfloat16),
             pltpu.VMEM(side, jnp.bfloat16),
@@ -412,6 +473,7 @@
             pltpu.VMEM((devices, width, PAIRS), jnp.float32),
             dma((1,)), dma((1,)), dma((1,)), dma((devices // 2 - 1,)),
             dma((devices,)), dma((devices,)), dma((1,)), dma((devices,)), dma((devices,)),
+            dma((1,)),
         ],
         compiler_params=pltpu.CompilerParams(collective_id=1, has_side_effects=True),
         name="screen_and_sum",
@@ -424,20 +486,17 @@
     twin_points = lax.ppermute(
         gsphere, "grid", [(g, (devices - g) % devices) for g in range(devices)]
     )
-    by_plane = jnp.transpose(valence, (1, 0, 2))
-    pieces = jnp.stack([
-        lax.dynamic_slice_in_dim(by_plane, blocks[b] % held_blocks * BLK, BLK, 1) for b in range(2)
-    ])
-    chosen = spread(blocks // held_blocks, pieces)
+    by_plane = jnp.transpose(valence, (1, 0, 2)).reshape(planes, held_blocks, BLK, LANES)
+    chosen = spread(blocks, by_plane)
     y_section = densities(
         chosen, jnp.transpose(conduction, (1, 0, 2)), jnp.asarray(z_matrix()), jnp.asarray(y_matrix())
     )
     blocks_y = y_section[:, :, : 2 * KF].reshape(planes, NEG, KF, 2, 2 * PAIRS)
     lowest = jnp.flip(y_section[:, :, 2 * KF :], axis=1)
     lowest = jnp.pad(lowest, ((0, 0), (0, KF - NEG), (0, 0), (0, 0)))
-    blocks_y = jnp.concatenate([blocks_y, lowest[:, None]], axis=1).transpose(2, 0, 3, 1, 4)
-    moved = lax.all_to_all(blocks_y, "grid", split_axis=0, concat_axis=0, tiled=True)
-    moved = moved.reshape(2 * GRID_N, NEG + 1, 2 * PAIRS).transpose(1, 0, 2)
+    blocks_y = jnp.concatenate([blocks_y, lowest[:, None]], axis=1).transpose(2, 0, 1, 3, 4)
+    moved = exchange(blocks_y, devices)
+    moved = moved.transpose(2, 0, 1, 3, 4).reshape(NEG + 1, 2 * GRID_N, 2 * PAIRS)
     qx, qz = gsphere // KF, gsphere % KF
     twin_qx, twin_qz = twin_points // KF, twin_points % KF
     own_at = jnp.where(qz < NEG, qz * ROWS_X + qx, -1)[:, None]

time: 147 us -> 140 us (0.952)
  Pallas kernels: 96.1 us -> 122 us
  waiting for transfers between devices: 15.2 us -> 0.01 us
  starting transfers between devices: 18.2 us -> 7.71 us
  between operations: 3.93 us -> 0.09 us
  other arithmetic: 3.95 us -> 1.77 us
  local copies, waits for them, and re-layouts: 9.13 us -> 7.63 us
    pallas_call x1 -> x2, Pallas kernels: 37.2 us -> 69.4 us  [the longest x1 35 us: exchange(): pl.pallas_call(functools.partial(exchange_kernel, devices), out_shape=jax...]
    ppermute x1, waiting for transfers between devices: 14.1 us -> 0.01 us  [per_device(): lax.ppermute(gsphere, 'grid', [(g, (devices - g) % devices) for g in rang...]
    all_to_all x1 -> x0, starting transfers between devices: 12.7 us -> none  [per_device(): lax.all_to_all(blocks_y, 'grid', split_axis=0, concat_axis=0, tiled=True)]
    pallas_call x1, Pallas kernels: 44.4 us -> 38.5 us  [tail(): pl.pallas_call(functools.partial(tail_kernel, devices), out_shape=jax.Sha...]
    transpose x0 -> x1, local copies, waits for them, and re-layouts: none -> 2.95 us  [per_device(): moved.transpose(2, 0, 1, 3, 4).reshape(NEG + 1, 2 * GRID_N, 2 * PAIRS)]
    ppermute x1, starting transfers between devices: 5.46 us -> 7.71 us  [per_device(): lax.ppermute(gsphere, 'grid', [(g, (devices - g) % devices) for g in rang...]
    all_to_all x1 -> x0, local copies, waits for them, and re-layouts: 1.78 us -> none  [per_device(): lax.all_to_all(blocks_y, 'grid', split_axis=0, concat_axis=0, tiled=True)]
  transfers between devices with their start and end apart: 2 -> 1, of which waited for: 2 -> 0; matrix products, arithmetic and copies ran while one was open for 2% -> 5% of each run, Pallas kernels for 0% -> 58%
where the time goes in v3:
time: 140 us
  Pallas kernels  122 us (87%)
  starting transfers between devices  7.71 us (6%)
  local copies, waits for them, and re-layouts  7.63 us (5%)
  other arithmetic  1.77 us (1%)
    pallas_call x1, Pallas kernels, tail(): pl.pallas_call(functools.partial(tail_kernel, devices), out_shape=jax.Sha...  38.5 us
    pallas_call x1, Pallas kernels, exchange(): pl.pallas_call(functools.partial(exchange_kernel, devices), out_shape=jax...  35 us
    pallas_call x1, Pallas kernels, spread(): pl.pallas_call(spread_kernel, out_shape=jax.ShapeDtypeStruct(whole, jnp.b...  34.4 us
    pallas_call x1, Pallas kernels, densities(): pl.pallas_call(density_kernel, grid=(planes,), out_shape=jax.ShapeDtypeSt...  12.1 us
    ppermute x1, starting transfers between devices, per_device(): lax.ppermute(gsphere, 'grid', [(g, (devices - g) % devices) for g in rang...  7.71 us
    transpose x1, local copies, waits for them, and re-layouts, per_device(): moved.transpose(2, 0, 1, 3, 4).reshape(NEG + 1, 2 * GRID_N, 2 * PAIRS)  2.95 us
  transfers between devices with their start and end apart: 1, of which 0 were waited for; matrix products, arithmetic and copies ran while one was open for 5% of the time, Pallas kernels for 58%

profile of v3, /device:TPU:1, one launch (start us, length us, event | category | flops | bytes accessed | tf_op | source)
XLA Modules:
  0.0 139.7 jit_solution(5588170031721017512)
XLA Ops:
  0.0 7.7 %collective-permute-start = (s32[192]{0:T(256)}, s32[192]{0:T(256)S(1)}, u32[]{:S(2)}, u32[]{:S(2)}) collective-permute-start(s32[192]{0:T(256)} %param.12), channel_id=1, source_target_pairs={{0,0},{1,31},{2,30},{3,29},{4,28},{5,27},{6,26},{7,25},{8,24},{9,2... | collective-permute-start | bytes 2312 | tf_op jit(solution)/shard_map/ppermute | solution.py:486
  7.7 34.4 %spread_blocks.1.chosen = bf16[2,3,8,9216]{3,2,1,0:T(8,128)(2,1)} custom-call(s32[2]{0:T(128)} %blocks_ref.1, bf16[3,2,8,9216]{3,2,1,0:T(8,128)(2,1)} %bitcast.18), custom_call_target="tpu_custom_call" | custom-call | tf_op jit(solution)/shard_map/spread_blocks/pallas_call | solution.py:169
  42.1 0.0 copy-start
  42.2 12.1 %pair_density.1 = bf16[3,17,66,128]{3,2,1,0:T(8,128)(2,1)} custom-call(bf16[2,3,8,9216]{3,2,1,0:T(8,128)(2,1)} %spread_blocks.1.chosen, bf16[3,8,9216]{2,1,0:T(8,128)(2,1)} %bitcast.19, bf16[136,384]{1,0:T(8,128)(2,1)} %constant.57.clone.z_mat, bf16[66,192]{1,0:T(8,128)(2,1)} %constant.58.clone.mix), custom_call_target="tpu_custom_call" | custom-call | tf_op jit(solution)/shard_map/pair_density/pallas_call | solution.py:217
  54.2 0.0 slice-start
  54.2 1.0 slice.9
  55.2 0.0 copy-done
  55.3 0.1 slice-done
  55.4 1.7 %maximum_bitcast_fusion.src = bf16[32,3,18,2,128]{4,3,2,1,0:T(2,128)(2,1)} fusion(bf16[3,1,32,2,128]{4,3,1,0,2:T(2,128)(2,1)S(1)} %pad_bitcast_fusion, bf16[3,17,32,2,128]{4,3,2,1,0:T(2,128)(2,1)S(1)} %bitcast.17), kind=kLoop, calls=%fused_computation | loop fusion | flops 1769472 | bytes 1769472 | tf_op jit(solution)/shard_map/transpose | solution.py:497
  57.2 35.0 %planes_for_frequencies.1 = bf16[32,3,18,2,128]{4,3,2,1,0:T(2,128)(2,1)} custom-call(bf16[32,3,18,2,128]{4,3,2,1,0:T(2,128)(2,1)} %maximum_bitcast_fusion.src), custom_call_target="tpu_custom_call" | custom-call | tf_op jit(solution)/shard_map/planes_for_frequencies/pallas_call | solution.py:265
  92.2 2.9 %copy.13 = bf16[18,32,3,2,128]{4,3,2,1,0:T(2,128)(2,1)} copy(bf16[18,32,3,2,128]{4,3,0,2,1:T(2,128)(2,1)} %bitcast.16) | data formatting | bytes 1769472 | tf_op jit(solution)/shard_map/transpose | solution.py:499
  95.1 0.8 copy.14.own_at
  95.9 0.8 copy.16.lone_at
  96.6 0.0 collective-permute-done
  96.7 0.8 copy.15.twin_at
  97.4 2.5 %x_and_sphere.1 = (bf16[192,256]{1,0:T(8,128)(2,1)}, bf16[192,256]{1,0:T(8,128)(2,1)}, bf16[32,256]{1,0:T(8,128)(2,1)}) custom-call(bf16[18,192,128]{2,1,0:T(8,128)(2,1)} %bitcast.15, bf16[96,192]{1,0:T(8,128)(2,1)} %constant.59.clone.mix, s32[192,1]{1,0:T(8,128)} %copy.14.own_at, s32[192,1]{1,0:T(8,128)} %copy.15.twin_at), custom_call_target="tpu_custom_call" | custom-call | tf_op jit(solution)/shard_map/x_and_sphere/pallas_call | solution.py:302
  100.0 38.5 %screen_and_sum.1 = f32[2,64]{1,0:T(2,128)} custom-call(bf16[192,256]{1,0:T(8,128)(2,1)} %get-tuple-element.8.own_rows, bf16[192,256]{1,0:T(8,128)(2,1)} %get-tuple-element.9.twin_rows, bf16[32,256]{1,0:T(8,128)(2,1)} %get-tuple-element.10.table, s32[192,1]{1,0:T(8,128)} %copy.16.lone_at, bf16[192,6144]{1,0:T(8,128)(2,1)} %screened.1), custom_call_target="tpu_custom_call" | custom-call | tf_op jit(solution)/shard_map/screen_and_sum/pallas_call | solution.py:459
  138.4 1.2 copy.21
  (6 shorter events, 0.1 us)
Async XLA Ops:
  0.0 96.6 %collective-permute-start = (s32[192]{0:T(256)}, s32[192]{0:T(256)S(1)}, u32[]{:S(2)}, u32[]{:S(2)}) collective-permute-start(s32[192]{0:T(256)} %param.12), channel_id=1, source_target_pairs={{0,0},{1,31},{2,30},{3,29},{4,28},{5,27},{6,26},{7,25},{8,24},{9,2... | collective-permute-start | bytes 2312 | tf_op jit(solution)/shard_map/ppermute | solution.py:486
  42.1 13.1 %copy-start = (s32[192]{0:T(256)S(1)}, s32[192]{0:T(256)}, u32[]{:S(2)}) copy-start(s32[192]{0:T(256)} %param.12) | copy-start | bytes 2308
  54.2 1.2 slice-start

commit v4 on v3

--- a/solution.py
+++ b/solution.py
@@ -187,97 +187,117 @@
     )(blocks, held_bands)
 
 
-def density_kernel(chosen, cond, z_mat, mix, out_ref, sections):
-    def step(j, carry):
-        both = []
-        for half in range(2):
-            at = pl.ds(pl.multiple_of((2 * j + half) * CHUNK, 128), CHUNK)
-            c = cond[0, :, at].astype(jnp.float32)
-            v = jnp.concatenate(
-                [chosen[0, 0, :, at].astype(jnp.float32), chosen[1, 0, :, at].astype(jnp.float32)]
-            )
-            dens = (v[:, None, :] * c[None, :, :]).reshape(2 * PAIRS, CHUNK).astype(jnp.bfloat16)
-            part = lax.dot_general(
-                z_mat[...], dens, (((1,), (1,)), ((), ())), preferred_element_type=jnp.float32
-            )
-            both.append(part.reshape(NEG, 2 * ROWS_Y, 2 * PAIRS))
-        joined = jnp.concatenate(both, axis=1).astype(jnp.bfloat16)
-        sections[:, pl.ds(pl.multiple_of(j * 4 * ROWS_Y, 16), 4 * ROWS_Y), :] = joined
-        return carry
-
-    lax.fori_loop(0, LANES // CHUNK // 2, step, 0)
-    for q in range(NEG):
-        out_ref[0, q] = jnp.dot(
-            mix[...], sections[q], preferred_element_type=jnp.float32
-        ).astype(jnp.bfloat16)
-
-
-def densities(chosen, cond, z_mat, mix):
-    planes = cond.shape[0]
-    return pl.pallas_call(
-        density_kernel,
-        grid=(planes,),
-        out_shape=jax.ShapeDtypeStruct((planes, NEG, 2 * KF + 2, 2 * PAIRS), jnp.bfloat16),
-        in_specs=[
-            pl.BlockSpec((2, 1, BLK, LANES), lambda i: (0, i, 0, 0)),
-            pl.BlockSpec((1, BLK, LANES), lambda i: (i, 0, 0)),
-            pl.BlockSpec(z_mat.shape, lambda i: (0, 0)),
-            pl.BlockSpec(mix.shape, lambda i: (0, 0)),
-        ],
-        out_specs=pl.BlockSpec((1, NEG, 2 * KF + 2, 2 * PAIRS), lambda i: (i, 0, 0, 0)),
-        scratch_shapes=[pltpu.VMEM((NEG, 2 * GRID_N, 2 * PAIRS), jnp.bfloat16)],
-        name="pair_density",
-    )(chosen, cond, z_mat, mix)
-
-
-def exchange_kernel(devices, src, out_ref, kept, send, recv, own):
+def density_kernel(
+    devices, chosen, cond, z_mat, mix, out_ref, sections, made, send, recv, own
+):
     me = lax.axis_index("grid")
     half = devices // 2
     ring = half // 2
     z, y, c = me // half, me % half // 2, me % 2
-    greet([{"grid": (me + k) % devices} for k in range(1, devices)])
-    inward = pltpu.make_async_copy(src.at[me], kept, own.at[0])
-    inward.start()
-    moves = []
-    for dy in sorted(range(ring), key=lambda d: -min(d, ring - d)):
-        for dz in (1, 0):
-            for dc in (0, 1):
-                k = dz * half + dy * 2 + dc
-                if k:
-                    peer = (z + dz) % 2 * half + (y + dy) % ring * 2 + (c + dc) % 2
-                    copy = remote(
-                        src.at[peer], out_ref.at[me], send.at[k], recv.at[k], {"grid": peer}
-                    )
-                    copy.start()
-                    moves.append((dy, dz, dc, k, copy))
-    inward.wait()
-    outward = pltpu.make_async_copy(kept, out_ref.at[me], own.at[1])
-    outward.start()
-    for dy, dz, dc, k, copy in moves:
-        copy.wait_send()
-        peer = (z + dz) % 2 * half + (y + ring - dy) % ring * 2 + (c + dc) % 2
-        remote(src.at[peer], out_ref.at[peer], send.at[k], recv.at[k], {"grid": peer}).wait_recv()
-    outward.wait()
-
-
-def exchange(blocks, devices):
+    planes = cond.shape[0]
+    barrier = pltpu.get_barrier_semaphore()
+    for k in range(1, devices):
+        pl.semaphore_signal(
+            barrier, inc=1, device_id={"grid": (me + k) % devices}, device_id_type=MESH
+        )
+
+    def compute(x):
+        def z_step(j, carry):
+            both = []
+            for part in range(2):
+                at = pl.ds(pl.multiple_of((2 * j + part) * CHUNK, 128), CHUNK)
+                cc = cond[x, :, at].astype(jnp.float32)
+                v = jnp.concatenate(
+                    [chosen[0, x, :, at].astype(jnp.float32), chosen[1, x, :, at].astype(jnp.float32)]
+                )
+                dens = (v[:, None, :] * cc[None, :, :]).reshape(2 * PAIRS, CHUNK)
+                summed = lax.dot_general(
+                    z_mat[...], dens.astype(jnp.bfloat16), (((1,), (1,)), ((), ())),
+                    preferred_element_type=jnp.float32,
+                )
+                both.append(summed.reshape(NEG, 2 * ROWS_Y, 2 * PAIRS))
+            joined = jnp.concatenate(both, axis=1).astype(jnp.bfloat16)
+            sections[:, pl.ds(pl.multiple_of(j * 4 * ROWS_Y, 16), 4 * ROWS_Y), :] = joined
+            return carry
+
+        lax.fori_loop(0, LANES // CHUNK // 2, z_step, 0)
+        made[x, :, NEG] = jnp.zeros((KF, 2, 2 * PAIRS), jnp.bfloat16)
+
+        for q in range(NEG):
+            value = jnp.dot(
+                mix[...], sections[q], preferred_element_type=jnp.float32
+            ).astype(jnp.bfloat16)
+            made[x, :, q] = value[: 2 * KF].reshape(KF, 2, 2 * PAIRS)
+            made[x, NEG - 1 - q, NEG] = value[2 * KF :]
+
+    def moves(x):
+        for dy in sorted(range(ring), key=lambda d: -min(d, ring - d)):
+            for dz in (1, 0):
+                for dc in (0, 1):
+                    k = dz * half + dy * 2 + dc
+                    if k:
+                        to = (z + dz) % 2 * half + (y + dy) % ring * 2 + (c + dc) % 2
+                        source = (z + dz) % 2 * half + (y + ring - dy) % ring * 2 + (c + dc) % 2
+                        yield k, to, source
+
+    def post(x):
+        for k, to, _ in moves(x):
+            remote(
+                made.at[x, to], out_ref.at[me, x], send.at[x, k], recv.at[x, k], {"grid": to}
+            ).start()
+        pltpu.make_async_copy(made.at[x, me], out_ref.at[me, x], own.at[x]).start()
+
+    compute(0)
+    pl.semaphore_wait(barrier, devices - 1)
+    post(0)
+
+    def plane(x, carry):
+        compute(x)
+        post(x)
+        return carry
+
+    lax.fori_loop(1, planes, plane, 0)
+
+    def finish(x, carry):
+        for k, to, source in moves(x):
+            remote(
+                made.at[x, to], out_ref.at[source, x], send.at[x, k], recv.at[x, k], {"grid": to}
+            ).wait()
+        pltpu.make_async_copy(made.at[x, me], out_ref.at[me, x], own.at[x]).wait()
+        return carry
+
+    lax.fori_loop(0, planes, finish, 0)
+
+
+def densities(chosen, cond, z_mat, mix, devices):
+    planes = cond.shape[0]
     dma = pltpu.SemaphoreType.DMA
+    vmem = pl.BlockSpec(memory_space=pltpu.VMEM)
     return pl.pallas_call(
-        functools.partial(exchange_kernel, devices),
-        out_shape=jax.ShapeDtypeStruct(blocks.shape, blocks.dtype),
-        in_specs=[pl.BlockSpec(memory_space=pl.ANY)],
+        functools.partial(density_kernel, devices),
+        out_shape=jax.ShapeDtypeStruct((devices, planes, NEG + 1, 2, 2 * PAIRS), jnp.bfloat16),
+        in_specs=[vmem] * 4,
         out_specs=pl.BlockSpec(memory_space=pl.ANY),
         scratch_shapes=[
-            pltpu.VMEM(blocks.shape[1:], blocks.dtype), dma((devices,)), dma((devices,)), dma((2,))
+            pltpu.VMEM((NEG, 2 * GRID_N, 2 * PAIRS), jnp.bfloat16),
+            pltpu.VMEM((planes, devices, NEG + 1, 2, 2 * PAIRS), jnp.bfloat16),
+            dma((planes, devices)), dma((planes, devices)), dma((planes,)),
         ],
         compiler_params=pltpu.CompilerParams(collective_id=2, has_side_effects=True),
-        name="planes_for_frequencies",
-    )(blocks)
+        name="density_and_exchange",
+    )(chosen, cond, z_mat, mix)
 
 
 def one_hot(index, count):
-    lanes = lax.broadcasted_iota(jnp.int32, (index.shape[0], count), 1)
-    return jnp.where(lanes == index, 1.0, 0.0).astype(jnp.bfloat16)
+    rows = lax.broadcasted_iota(jnp.int32, (count, index.shape[1]), 0)
+    return jnp.where(rows == index, 1.0, 0.0).astype(jnp.bfloat16)
+
+
+def pick(index, table):
+    return lax.dot_general(
+        one_hot(index, table.shape[0]), table, (((0,), (0,)), ((), ())),
+        preferred_element_type=jnp.float32,
+    )
 
 
 def sphere_kernel(moved, mix, own_at, twin_at, own_ref, twin_ref, table_ref, table):
@@ -288,16 +308,14 @@
             table[q * ROWS_X : (q + 1) * ROWS_X] = both
         else:
             table_ref[...] = both[:KF]
-    count = table.shape[0]
-    own = jnp.dot(one_hot(own_at[...], count), table[...], preferred_element_type=jnp.float32)
-    own_ref[...] = own.astype(jnp.bfloat16)
-    twin = jnp.dot(one_hot(twin_at[...], count), table[...], preferred_element_type=jnp.float32)
+    own_ref[...] = pick(own_at[...], table[...]).astype(jnp.bfloat16)
+    twin = pick(twin_at[...], table[...])
     lanes = lax.broadcasted_iota(jnp.int32, twin.shape, 1)
     twin_ref[...] = jnp.where(lanes < 2 * PAIRS, twin, -twin).astype(jnp.bfloat16)
 
 
 def spheres(moved, mix, own_at, twin_at):
-    rows = jax.ShapeDtypeStruct((own_at.shape[0], 4 * PAIRS), jnp.bfloat16)
+    rows = jax.ShapeDtypeStruct((own_at.shape[1], 4 * PAIRS), jnp.bfloat16)
     vmem = pl.BlockSpec(memory_space=pltpu.VMEM)
     return pl.pallas_call(
         sphere_kernel,
@@ -353,10 +371,7 @@
                 table, tables.at[i], lone_send.at[0], lone_recv.at[i], {"grid": i + 1}
             ).wait_recv()
         count = (half - 1) * KF
-        picked = jnp.dot(
-            one_hot(lone_at[...], count), tables[...].reshape(count, 4 * PAIRS),
-            preferred_element_type=jnp.float32,
-        )
+        picked = pick(lone_at[...], tables[...].reshape(count, 4 * PAIRS))
         got[...] = picked.astype(jnp.bfloat16)
 
     @pl.when(helper)
@@ -488,20 +503,16 @@
     )
     by_plane = jnp.transpose(valence, (1, 0, 2)).reshape(planes, held_blocks, BLK, LANES)
     chosen = spread(blocks, by_plane)
-    y_section = densities(
-        chosen, jnp.transpose(conduction, (1, 0, 2)), jnp.asarray(z_matrix()), jnp.asarray(y_matrix())
-    )
-    blocks_y = y_section[:, :, : 2 * KF].reshape(planes, NEG, KF, 2, 2 * PAIRS)
-    lowest = jnp.flip(y_section[:, :, 2 * KF :], axis=1)
-    lowest = jnp.pad(lowest, ((0, 0), (0, KF - NEG), (0, 0), (0, 0)))
-    blocks_y = jnp.concatenate([blocks_y, lowest[:, None]], axis=1).transpose(2, 0, 1, 3, 4)
-    moved = exchange(blocks_y, devices)
+    moved = densities(
+        chosen, jnp.transpose(conduction, (1, 0, 2)), jnp.asarray(z_matrix()),
+        jnp.asarray(y_matrix()), devices,
+    )
     moved = moved.transpose(2, 0, 1, 3, 4).reshape(NEG + 1, 2 * GRID_N, 2 * PAIRS)
     qx, qz = gsphere // KF, gsphere % KF
     twin_qx, twin_qz = twin_points // KF, twin_points % KF
-    own_at = jnp.where(qz < NEG, qz * ROWS_X + qx, -1)[:, None]
-    lone_at = jnp.where(qz < NEG, -1, (qz - NEG) * KF + qx)[:, None]
-    twin_at = jnp.where(twin_qz < NEG, -1, (KF - twin_qz) * ROWS_X + KF - twin_qx)[:, None]
+    own_at = jnp.where(qz < NEG, qz * ROWS_X + qx, -1)[None]
+    lone_at = jnp.where(qz < NEG, -1, (qz - NEG) * KF + qx)[None]
+    twin_at = jnp.where(twin_qz < NEG, -1, (KF - twin_qz) * ROWS_X + KF - twin_qx)[None]
     own_rows, twin_rows, table = spheres(moved, jnp.asarray(x_matrix()), own_at, twin_at)
     return tail(own_rows, twin_rows, table, lone_at, screened, devices)[None]
 

time: 140 us -> 128 us (0.914)
  Pallas kernels: 122 us -> 112 us
  local copies, waits for them, and re-layouts: 7.63 us -> 4.18 us
    pallas_call x2 -> x1, Pallas kernels: 47.1 us -> 37.9 us  [densities(): pl.pallas_call(functools.partial(density_kernel, devices), out_shape=jax....]
    select_n x3, other arithmetic: 0.04 us -> 3.13 us  [the longest x1 1.28 us: per_device(): own_at = jnp.where(qz < NEG, qz * ROWS_X + qx, -1)[None]]
    broadcast_in_dim x4 -> x0, local copies, waits for them, and re-layouts: 2.32 us -> none  [the longest x1 0.77 us: per_device(): jnp.where(twin_qz < NEG, -1, (KF - twin_qz) * ROWS_X + KF - twin_qx)]
    transpose x1 -> x0, other arithmetic: 1.73 us -> none  [per_device(): jnp.concatenate([blocks_y, lowest[:, None]], axis=1)]
  transfers between devices with their start and end apart: 1 -> 1, of which waited for: 0 -> 0; matrix products, arithmetic and copies ran while one was open for 5% -> 4% of each run, Pallas kernels for 58% -> 57%
where the time goes in v4:
time: 128 us; the launch traced here: 127 us
  Pallas kernels  112 us (88%)
  starting transfers between devices  7.71 us (6%)
  local copies, waits for them, and re-layouts  4.18 us (3%)
  other arithmetic  3.13 us (2%)
    pallas_call x1, Pallas kernels, densities(): pl.pallas_call(functools.partial(density_kernel, devices), out_shape=jax....  37.9 us
    pallas_call x1, Pallas kernels, tail(): pl.pallas_call(functools.partial(tail_kernel, devices), out_shape=jax.Sha...  37.5 us
    pallas_call x1, Pallas kernels, spread(): pl.pallas_call(spread_kernel, out_shape=jax.ShapeDtypeStruct(whole, jnp.b...  34.4 us
    ppermute x1, starting transfers between devices, per_device(): lax.ppermute(gsphere, 'grid', [(g, (devices - g) % devices) for g in rang...  7.71 us
    transpose x1, local copies, waits for them, and re-layouts, per_device(): moved.transpose(2, 0, 1, 3, 4).reshape(NEG + 1, 2 * GRID_N, 2 * PAIRS)  2.95 us
  transfers between devices with their start and end apart: 1, of which 0 were waited for; matrix products, arithmetic and copies ran while one was open for 4% of the time, Pallas kernels for 57%

profile of v4, /device:TPU:1, one launch (start us, length us, event | category | flops | bytes accessed | tf_op | source)
XLA Modules:
  0.0 127.3 jit_solution(9226472278345925529)
XLA Ops:
  0.0 7.7 %collective-permute-start = (s32[192]{0:T(256)}, s32[192]{0:T(256)S(1)}, u32[]{:S(2)}, u32[]{:S(2)}) collective-permute-start(s32[192]{0:T(256)} %param.12), channel_id=1, source_target_pairs={{0,0},{1,31},{2,30},{3,29},{4,28},{5,27},{6,26},{7,25},{8,24},{9,2... | collective-permute-start | bytes 2312 | tf_op jit(solution)/shard_map/ppermute | solution.py:501
  7.7 1.3 add_select_fusion
  9.0 1.3 %add_select_fusion.1 = s32[192]{0:T(256)} fusion(s32[192]{0:T(256)S(1)} %get-tuple-element.12, s32[192]{0:T(256)} %param.12), kind=kLoop, calls=%fused_computation.13 | loop fusion | flops 2880 | bytes 2304 | tf_op jit(solution)/shard_map/jit(_where)/select_n | solution.py:513
  10.3 34.4 %spread_blocks.1.chosen = bf16[2,3,8,9216]{3,2,1,0:T(8,128)(2,1)} custom-call(s32[2]{0:T(128)} %blocks_ref.1, bf16[3,2,8,9216]{3,2,1,0:T(8,128)(2,1)} %bitcast.12), custom_call_target="tpu_custom_call" | custom-call | tf_op jit(solution)/shard_map/spread_blocks/pallas_call | solution.py:169
  44.7 37.9 %density_and_exchange.1 = bf16[32,3,18,2,128]{4,3,2,1,0:T(2,128)(2,1)} custom-call(bf16[2,3,8,9216]{3,2,1,0:T(8,128)(2,1)} %spread_blocks.1.chosen, bf16[3,8,9216]{2,1,0:T(8,128)(2,1)} %bitcast.13, bf16[136,384]{1,0:T(8,128)(2,1)} %constant.54.clone.z_mat, bf16[66,192]{1,0:T(8,128)(2,1)} %constant.55.clone.mix), custom_call_target="tpu_custom_call" | custom-call | tf_op jit(solution)/shard_map/density_and_exchange/pallas_call | solution.py:276
  82.5 2.9 %copy.9 = bf16[18,32,3,2,128]{4,3,2,1,0:T(2,128)(2,1)} copy(bf16[18,32,3,2,128]{4,3,0,2,1:T(2,128)(2,1)} %bitcast.11) | data formatting | bytes 1769472 | tf_op jit(solution)/shard_map/transpose | solution.py:510
  85.5 0.0 collective-permute-done
  85.5 0.6 compare_select_fusion
  86.1 2.5 %x_and_sphere.1 = (bf16[192,256]{1,0:T(8,128)(2,1)}, bf16[192,256]{1,0:T(8,128)(2,1)}, bf16[32,256]{1,0:T(8,128)(2,1)}) custom-call(bf16[18,192,128]{2,1,0:T(8,128)(2,1)} %bitcast.10, bf16[96,192]{1,0:T(8,128)(2,1)} %constant.56.clone.mix, s32[1,192]{1,0:T(1,128)} %bitcast.15, s32[1,192]{1,0:T(1,128)} %bitcast.16), custom_call_target="tpu_custom_call" | custom-call | tf_op jit(solution)/shard_map/x_and_sphere/pallas_call | solution.py:320
  88.6 37.5 %screen_and_sum.1 = f32[2,64]{1,0:T(2,128)} custom-call(bf16[192,256]{1,0:T(8,128)(2,1)} %get-tuple-element.8.own_rows, bf16[192,256]{1,0:T(8,128)(2,1)} %get-tuple-element.9.twin_rows, bf16[32,256]{1,0:T(8,128)(2,1)} %get-tuple-element.10.table, s32[1,192]{1,0:T(1,128)} %bitcast.14, bf16[192,6144]{1,0:T(8,128)(2,1)} %screened.1), custom_call_target="tpu_custom_call" | custom-call | tf_op jit(solution)/shard_map/screen_and_sum/pallas_call | solution.py:474
  126.1 1.2 copy.11
Async XLA Ops:
  0.0 85.5 %collective-permute-start = (s32[192]{0:T(256)}, s32[192]{0:T(256)S(1)}, u32[]{:S(2)}, u32[]{:S(2)}) collective-permute-start(s32[192]{0:T(256)} %param.12), channel_id=1, source_target_pairs={{0,0},{1,31},{2,30},{3,29},{4,28},{5,27},{6,26},{7,25},{8,24},{9,2... | collective-permute-start | bytes 2312 | tf_op jit(solution)/shard_map/ppermute | solution.py:501

commit v5 on v4

--- a/solution.py
+++ b/solution.py
@@ -188,7 +188,8 @@
 
 
 def density_kernel(
-    devices, chosen, cond, z_mat, mix, out_ref, sections, made, send, recv, own
+    devices, chosen, cond, z_mat, mix, points, out_ref, twin_points, sections, made,
+    send, recv, own, point_send, point_recv,
 ):
     me = lax.axis_index("grid")
     half = devices // 2
@@ -250,6 +251,20 @@
     compute(0)
     pl.semaphore_wait(barrier, devices - 1)
     post(0)
+    paired = (me != 0) & (me != half)
+    swap = remote(
+        points, twin_points, point_send.at[0], point_recv.at[0], {"grid": (devices - me) % devices}
+    )
+    keep = pltpu.make_async_copy(points, twin_points, point_send.at[0])
+
+    @pl.when(paired)
+    def _():
+        swap.start()
+
+    @pl.when(jnp.logical_not(paired))
+    def _():
+        keep.start()
+        keep.wait()
 
     def plane(x, carry):
         compute(x)
@@ -268,24 +283,32 @@
 
     lax.fori_loop(0, planes, finish, 0)
 
-
-def densities(chosen, cond, z_mat, mix, devices):
+    @pl.when(paired)
+    def _():
+        swap.wait()
+
+
+def densities(chosen, cond, z_mat, mix, points, devices):
     planes = cond.shape[0]
     dma = pltpu.SemaphoreType.DMA
     vmem = pl.BlockSpec(memory_space=pltpu.VMEM)
+    anywhere = pl.BlockSpec(memory_space=pl.ANY)
     return pl.pallas_call(
         functools.partial(density_kernel, devices),
-        out_shape=jax.ShapeDtypeStruct((devices, planes, NEG + 1, 2, 2 * PAIRS), jnp.bfloat16),
-        in_specs=[vmem] * 4,
-        out_specs=pl.BlockSpec(memory_space=pl.ANY),
+        out_shape=[
+            jax.ShapeDtypeStruct((devices, planes, NEG + 1, 2, 2 * PAIRS), jnp.bfloat16),
+            jax.ShapeDtypeStruct(points.shape, points.dtype),
+        ],
+        in_specs=[vmem] * 4 + [anywhere],
+        out_specs=[anywhere] * 2,
         scratch_shapes=[
             pltpu.VMEM((NEG, 2 * GRID_N, 2 * PAIRS), jnp.bfloat16),
             pltpu.VMEM((planes, devices, NEG + 1, 2, 2 * PAIRS), jnp.bfloat16),
-            dma((planes, devices)), dma((planes, devices)), dma((planes,)),
+            dma((planes, devices)), dma((planes, devices)), dma((planes,)), dma((1,)), dma((1,)),
         ],
         compiler_params=pltpu.CompilerParams(collective_id=2, has_side_effects=True),
         name="density_and_exchange",
-    )(chosen, cond, z_mat, mix)
+    )(chosen, cond, z_mat, mix, points)
 
 
 def one_hot(index, count):
@@ -300,36 +323,29 @@
     )
 
 
-def sphere_kernel(moved, mix, own_at, twin_at, own_ref, twin_ref, table_ref, table):
+def sphere_rows(moved, mix, points, twin_points, own_rows, twin_rows, table_ref, table):
     for q in range(NEG + 1):
-        part = jnp.dot(mix[...], moved[q], preferred_element_type=jnp.float32)
+        rows = moved[:, :, q].reshape(2 * GRID_N, 2 * PAIRS)
+        part = jnp.dot(mix[...], rows, preferred_element_type=jnp.float32)
         both = jnp.concatenate([part[:ROWS_X], part[ROWS_X:]], axis=1).astype(jnp.bfloat16)
         if q < NEG:
             table[q * ROWS_X : (q + 1) * ROWS_X] = both
         else:
             table_ref[...] = both[:KF]
-    own_ref[...] = pick(own_at[...], table[...]).astype(jnp.bfloat16)
-    twin = pick(twin_at[...], table[...])
+    qx, qz = lax.div(points, KF), lax.rem(points, KF)
+    twin_qx, twin_qz = lax.div(twin_points, KF), lax.rem(twin_points, KF)
+    own_at = jnp.where(qz < NEG, qz * ROWS_X + qx, -1)
+    twin_at = jnp.where(twin_qz < NEG, -1, (KF - twin_qz) * ROWS_X + KF - twin_qx)
+    own_rows[...] = pick(own_at, table[...]).astype(jnp.bfloat16)
+    twin = pick(twin_at, table[...])
     lanes = lax.broadcasted_iota(jnp.int32, twin.shape, 1)
-    twin_ref[...] = jnp.where(lanes < 2 * PAIRS, twin, -twin).astype(jnp.bfloat16)
-
-
-def spheres(moved, mix, own_at, twin_at):
-    rows = jax.ShapeDtypeStruct((own_at.shape[1], 4 * PAIRS), jnp.bfloat16)
-    vmem = pl.BlockSpec(memory_space=pltpu.VMEM)
-    return pl.pallas_call(
-        sphere_kernel,
-        out_shape=[rows, rows, jax.ShapeDtypeStruct((KF, 4 * PAIRS), jnp.bfloat16)],
-        in_specs=[vmem] * 4,
-        out_specs=[vmem] * 3,
-        scratch_shapes=[pltpu.VMEM((NEG * ROWS_X, 4 * PAIRS), jnp.bfloat16)],
-        name="x_and_sphere",
-    )(moved, mix, own_at, twin_at)
+    twin_rows[...] = jnp.where(lanes < 2 * PAIRS, twin, -twin).astype(jnp.bfloat16)
+    return jnp.where(qz < NEG, -1, (qz - NEG) * KF + qx)
 
 
 def tail_kernel(
-    devices, own_rows, twin_rows, table, lone_at, screened, out_ref,
-    weights, total, got, tables, side_a, side_b, rows, parts, arrived,
+    devices, moved, mix, points, twin_points, screened, out_ref,
+    own_rows, twin_rows, table, found, weights, total, got, tables, side_a, side_b, rows, parts, arrived,
     swap_send, swap_recv, lone_send, lone_recv, send, recv, own, sum_send, sum_recv, fetched,
 ):
     fetch = pltpu.make_async_copy(screened, weights, fetched.at[0])
@@ -342,7 +358,15 @@
     def at(zz, yy, cc):
         return zz * half + yy % ring * 2 + cc
 
-    greet([{"grid": (me + k) % devices} for k in range(1, devices)])
+    barrier = pltpu.get_barrier_semaphore()
+    for k in range(1, devices):
+        pl.semaphore_signal(
+            barrier, inc=1, device_id={"grid": (me + k) % devices}, device_id_type=MESH
+        )
+    lone_at = sphere_rows(
+        moved, mix, points[...], twin_points[...], own_rows, twin_rows, table, found
+    )
+    pl.semaphore_wait(barrier, devices - 1)
     paired = (me != 0) & (me != half)
     swap = remote(
         twin_rows, got, swap_send.at[0], swap_recv.at[0], {"grid": (devices - me) % devices}
@@ -371,7 +395,7 @@
                 table, tables.at[i], lone_send.at[0], lone_recv.at[i], {"grid": i + 1}
             ).wait_recv()
         count = (half - 1) * KF
-        picked = pick(lone_at[...], tables[...].reshape(count, 4 * PAIRS))
+        picked = pick(lone_at, tables[...].reshape(count, 4 * PAIRS))
         got[...] = picked.astype(jnp.bfloat16)
 
     @pl.when(helper)
@@ -466,21 +490,27 @@
     out_ref[...] = result
 
 
-def tail(own_rows, twin_rows, table, lone_at, screened, devices):
+def tail(moved, mix, points, twin_points, screened, devices):
     vmem = pl.BlockSpec(memory_space=pltpu.VMEM)
     dma = pltpu.SemaphoreType.DMA
     width = PAIRS // devices
-    side = (own_rows.shape[0], 2 * PAIRS)
+    side = (points.shape[1], 2 * PAIRS)
+    both = (points.shape[1], 4 * PAIRS)
+    table = (KF, 4 * PAIRS)
     return pl.pallas_call(
         functools.partial(tail_kernel, devices),
         out_shape=jax.ShapeDtypeStruct((width, PAIRS), jnp.float32),
         in_specs=[vmem] * 4 + [pl.BlockSpec(memory_space=pl.ANY)],
         out_specs=vmem,
         scratch_shapes=[
+            pltpu.VMEM(both, jnp.bfloat16),
+            pltpu.VMEM(both, jnp.bfloat16),
+            pltpu.VMEM(table, jnp.bfloat16),
+            pltpu.VMEM((NEG * ROWS_X, 4 * PAIRS), jnp.bfloat16),
             pltpu.VMEM(screened.shape, jnp.bfloat16),
             pltpu.VMEM(side, jnp.float32),
-            pltpu.VMEM(own_rows.shape, jnp.bfloat16),
-            pltpu.VMEM((devices // 2 - 1, *table.shape), jnp.bfloat16),
+            pltpu.VMEM(both, jnp.bfloat16),
+            pltpu.VMEM((devices // 2 - 1, *table), jnp.bfloat16),
             pltpu.VMEM(side, jnp.bfloat16),
             pltpu.VMEM(side, jnp.bfloat16),
             pltpu.VMEM((devices, *side), jnp.bfloat16),
@@ -492,29 +522,20 @@
         ],
         compiler_params=pltpu.CompilerParams(collective_id=1, has_side_effects=True),
         name="screen_and_sum",
-    )(own_rows, twin_rows, table, lone_at, screened)
+    )(moved, mix, points, twin_points, screened)
 
 
 def per_device(devices, valence, conduction, screened, blocks, gsphere):
     held_blocks = valence.shape[0] // BLK
     planes = conduction.shape[1]
-    twin_points = lax.ppermute(
-        gsphere, "grid", [(g, (devices - g) % devices) for g in range(devices)]
-    )
     by_plane = jnp.transpose(valence, (1, 0, 2)).reshape(planes, held_blocks, BLK, LANES)
     chosen = spread(blocks, by_plane)
-    moved = densities(
+    points = gsphere[None]
+    moved, twin_points = densities(
         chosen, jnp.transpose(conduction, (1, 0, 2)), jnp.asarray(z_matrix()),
-        jnp.asarray(y_matrix()), devices,
-    )
-    moved = moved.transpose(2, 0, 1, 3, 4).reshape(NEG + 1, 2 * GRID_N, 2 * PAIRS)
-    qx, qz = gsphere // KF, gsphere % KF
-    twin_qx, twin_qz = twin_points // KF, twin_points % KF
-    own_at = jnp.where(qz < NEG, qz * ROWS_X + qx, -1)[None]
-    lone_at = jnp.where(qz < NEG, -1, (qz - NEG) * KF + qx)[None]
-    twin_at = jnp.where(twin_qz < NEG, -1, (KF - twin_qz) * ROWS_X + KF - twin_qx)[None]
-    own_rows, twin_rows, table = spheres(moved, jnp.asarray(x_matrix()), own_at, twin_at)
-    return tail(own_rows, twin_rows, table, lone_at, screened, devices)[None]
+        jnp.asarray(y_matrix()), points, devices,
+    )
+    return tail(moved, jnp.asarray(x_matrix()), points, twin_points, screened, devices)[None]
 
 
 def solution(mesh):

time: 128 us -> 113 us (0.88)
  starting transfers between devices: 7.71 us -> 0 us
  other arithmetic: 3.13 us -> 0 us
  local copies, waits for them, and re-layouts: 4.18 us -> 1.23 us
    ppermute x1 -> x0, starting transfers between devices: 7.71 us -> none  [per_device(): lax.ppermute(gsphere, 'grid', [(g, (devices - g) % devices) for g in rang...]
    pallas_call x2 -> x1, Pallas kernels: 40.4 us -> 35.3 us  [densities(): pl.pallas_call(functools.partial(density_kernel, devices), out_shape=[jax...]
    select_n x3 -> x0, other arithmetic: 3.13 us -> none  [the longest x1 1.28 us: per_device(): own_at = jnp.where(qz < NEG, qz * ROWS_X + qx, -1)[None]]
    transpose x1 -> x0, local copies, waits for them, and re-layouts: 2.95 us -> none  [per_device(): moved.transpose(2, 0, 1, 3, 4).reshape(NEG + 1, 2 * GRID_N, 2 * PAIRS)]
    pallas_call x1, Pallas kernels: 34.4 us -> 37.2 us  [spread(): pl.pallas_call(spread_kernel, out_shape=jax.ShapeDtypeStruct(whole, jnp.b...]
    pallas_call x1, Pallas kernels: 37.5 us -> 39.2 us  [tail(): pl.pallas_call(functools.partial(tail_kernel, devices), out_shape=jax.Sha...]
  transfers between devices with their start and end apart: 1 -> 0, of which waited for: 0 -> 0; matrix products, arithmetic and copies ran while one was open for 4% -> 0% of each run, Pallas kernels for 57% -> 0%
where the time goes in v5:
time: 113 us
  Pallas kernels  112 us (99%)
  local copies, waits for them, and re-layouts  1.23 us (1%)
    pallas_call x1, Pallas kernels, tail(): pl.pallas_call(functools.partial(tail_kernel, devices), out_shape=jax.Sha...  39.2 us
    pallas_call x1, Pallas kernels, spread(): pl.pallas_call(spread_kernel, out_shape=jax.ShapeDtypeStruct(whole, jnp.b...  37.2 us
    pallas_call x1, Pallas kernels, densities(): pl.pallas_call(functools.partial(density_kernel, devices), out_shape=[jax...  35.3 us

profile of v5, /device:TPU:1, one launch (start us, length us, event | category | flops | bytes accessed | tf_op | source)
XLA Modules:
  0.0 113.0 jit_solution(10862652328182892933)
XLA Ops:
  0.0 37.2 %spread_blocks.1.chosen = bf16[2,3,8,9216]{3,2,1,0:T(8,128)(2,1)} custom-call(s32[2]{0:T(128)} %blocks_ref.1, bf16[3,2,8,9216]{3,2,1,0:T(8,128)(2,1)} %bitcast.6), custom_call_target="tpu_custom_call" | custom-call | tf_op jit(solution)/shard_map/spread_blocks/pallas_call | solution.py:169
  37.2 35.3 %density_and_exchange.1 = (bf16[32,3,18,2,128]{4,3,2,1,0:T(2,128)(2,1)}, s32[1,192]{1,0:T(1,128)}) custom-call(bf16[2,3,8,9216]{3,2,1,0:T(8,128)(2,1)} %spread_blocks.1.chosen, bf16[3,8,9216]{2,1,0:T(8,128)(2,1)} %bitcast.7, bf16[136,384]{1,0:T(8,128)(2,1)} %constant.6.clone.z_mat, bf16[66,192]{1,0:T(8,128)(2,1)} %constant.7.clone.mix, s32[1,192]{1,0:T(1,128)} %bitcast.8), custom_call_target="tpu_custom_call" | custom-call | tf_op jit(solution)/shard_map/density_and_exchange/pallas_call | solution.py:296
  72.5 39.2 %screen_and_sum.1 = f32[2,64]{1,0:T(2,128)} custom-call(bf16[32,3,18,2,128]{4,3,2,1,0:T(2,128)(2,1)} %get-tuple-element.7.moved, bf16[96,192]{1,0:T(8,128)(2,1)} %constant.8.clone.mix, s32[1,192]{1,0:T(1,128)} %bitcast.9, s32[1,192]{1,0:T(1,128)} %get-tuple-element.8.twin_points, bf16[192,6144]{1,0:T(8,128)(2,1)} %screened.1), custom_call_target="tpu_custom_call" | custom-call | tf_op jit(solution)/shard_map/screen_and_sum/pallas_call | solution.py:500
  111.8 1.2 %copy.10 = f32[1,2,64]{2,1,0:T(2,128)} copy(f32[1,2,64]{2,1,0:T(2,128)} %bitcast.10) | data formatting | bytes 1024

commit v6 on v5

--- a/solution.py
+++ b/solution.py
@@ -82,7 +82,7 @@
 
 def spread_kernel(
     blocks_ref, held_bands, out_ref, src, near0, near1, near2, near3, held, far, mine, full,
-    send1, recv1, own1, send2, recv2, send3, recv3, send4, recv4,
+    send1, recv1, own1, relay, relay_send, relay_recv, send2, recv2, send3, recv3, send4, recv4,
 ):
     band = lax.axis_index("band")
     z, x = band // SIDE, band % SIDE
@@ -105,7 +105,15 @@
     first = {}
     for j in order:
         s = (z + j) % SIDE
-        for k in (2, 1, 3):
+        way = 1 if j in (1, 2) else 3
+        q = (x + 2) % SIDE
+        copy = remote(
+            src.at[q // 2, :, :, lanes(q, s)], relay.at[j],
+            relay_send.at[j], relay_recv.at[j], along_x(way),
+        )
+        copy.start()
+        first[j, "relay"] = copy
+        for k in (1, 3):
             q = (x + k) % SIDE
             copy = remote(
                 src.at[q // 2, :, :, lanes(q, s)], near[j].at[x],
@@ -119,7 +127,21 @@
     owner = lax.div(blocks_ref[x // 2], count)
     owner_z, owner_x = owner // SIDE, owner % SIDE
     second = []
-    for j in order:
+
+    def forward(j):
+        way = 1 if j in (1, 2) else 3
+        first[j, "relay"].wait()
+        copy = remote(
+            relay.at[j], near[j].at[(x + SIDE - way) % SIDE],
+            send1.at[j, 1], recv1.at[j, 1], along_x(way),
+        )
+        copy.start()
+        first[j, 2] = copy
+
+    forward(order[0])
+    for i, j in enumerate(order):
+        if i + 1 < SIDE:
+            forward(order[i + 1])
         for k in range(SIDE):
             first[j, k].wait()
         if j == 0:
@@ -149,13 +171,28 @@
             third[j].wait()
         s = (z + SIDE - j) % SIDE
         part = full.at[x // 2, :, :, lanes(x, s)]
-        for k in (2, 1, 3):
+        for k in (1, 3):
             copy = remote(
                 mine if j == 0 else part, part, send4.at[j, k - 1], recv4.at[j, k - 1], along_x(k)
             )
             copy.start()
-            fourth.append(copy)
-    for copy in fourth:
+            fourth.append((j, k, copy))
+    passed = []
+    for j in (0, 1, 3, 2):
+        way = 1 if j in (0, 1) else 3
+        came = (x + SIDE - way) % SIDE
+        part = full.at[came // 2, :, :, lanes(came, (z + SIDE - j) % SIDE)]
+        remote(
+            part, part, send4.at[j, way - 1], recv4.at[j, way - 1], along_x(way)
+        ).wait_recv()
+        copy = remote(part, part, send4.at[j, 1], recv4.at[j, 1], along_x(way))
+        copy.start()
+        passed.append(copy)
+    for j, k, copy in fourth:
+        copy.wait_send()
+        if k != (1 if j in (0, 1) else 3):
+            copy.wait_recv()
+    for copy in passed:
         copy.wait()
     out_ref[...] = full[...]
 
@@ -179,6 +216,7 @@
             pltpu.VMEM(piece, jnp.bfloat16),
             pltpu.VMEM(whole, jnp.bfloat16),
             dma((SIDE, 3)), dma((SIDE, 3)), dma((SIDE,)),
+            pltpu.VMEM((SIDE, *piece), jnp.bfloat16), dma((SIDE,)), dma((SIDE,)),
             dma((3,)), dma((3,)), dma((3,)), dma((3,)),
             dma((SIDE, 3)), dma((SIDE, 3)),
         ],

time: 113 us -> 118 us (1.044)
  Pallas kernels: 112 us -> 116 us
    pallas_call x1, Pallas kernels: 37.2 us -> 43.3 us  [spread(): pl.pallas_call(spread_kernel, out_shape=jax.ShapeDtypeStruct(whole, jnp.b...]
where the time goes in v6:
time: 118 us
  Pallas kernels  116 us (98%)
  local copies, waits for them, and re-layouts  1.23 us (1%)
    pallas_call x1, Pallas kernels, spread(): pl.pallas_call(spread_kernel, out_shape=jax.ShapeDtypeStruct(whole, jnp.b...  43.3 us
    pallas_call x1, Pallas kernels, tail(): pl.pallas_call(functools.partial(tail_kernel, devices), out_shape=jax.Sha...  38.5 us
    pallas_call x1, Pallas kernels, densities(): pl.pallas_call(functools.partial(density_kernel, devices), out_shape=[jax...  34.6 us

profile of v6, /device:TPU:1, one launch (start us, length us, event | category | flops | bytes accessed | tf_op | source)
XLA Modules:
  0.0 117.6 jit_solution(9021443381081149702)
XLA Ops:
  0.0 43.3 %spread_blocks.1.chosen = bf16[2,3,8,9216]{3,2,1,0:T(8,128)(2,1)} custom-call(s32[2]{0:T(128)} %blocks_ref.1, bf16[3,2,8,9216]{3,2,1,0:T(8,128)(2,1)} %bitcast.6), custom_call_target="tpu_custom_call" | custom-call | tf_op jit(solution)/shard_map/spread_blocks/pallas_call | solution.py:206
  43.3 34.6 %density_and_exchange.1 = (bf16[32,3,18,2,128]{4,3,2,1,0:T(2,128)(2,1)}, s32[1,192]{1,0:T(1,128)}) custom-call(bf16[2,3,8,9216]{3,2,1,0:T(8,128)(2,1)} %spread_blocks.1.chosen, bf16[3,8,9216]{2,1,0:T(8,128)(2,1)} %bitcast.7, bf16[136,384]{1,0:T(8,128)(2,1)} %constant.6.clone.z_mat, bf16[66,192]{1,0:T(8,128)(2,1)} %constant.7.clone.mix, s32[1,192]{1,0:T(1,128)} %bitcast.8), custom_call_target="tpu_custom_call" | custom-call | tf_op jit(solution)/shard_map/density_and_exchange/pallas_call | solution.py:334
  77.9 38.5 %screen_and_sum.1 = f32[2,64]{1,0:T(2,128)} custom-call(bf16[32,3,18,2,128]{4,3,2,1,0:T(2,128)(2,1)} %get-tuple-element.7.moved, bf16[96,192]{1,0:T(8,128)(2,1)} %constant.8.clone.mix, s32[1,192]{1,0:T(1,128)} %bitcast.9, s32[1,192]{1,0:T(1,128)} %get-tuple-element.8.twin_points, bf16[192,6144]{1,0:T(8,128)(2,1)} %screened.1), custom_call_target="tpu_custom_call" | custom-call | tf_op jit(solution)/shard_map/screen_and_sum/pallas_call | solution.py:538
  116.4 1.2 %copy.10 = f32[1,2,64]{2,1,0:T(2,128)} copy(f32[1,2,64]{2,1,0:T(2,128)} %bitcast.10) | data formatting | bytes 1024

commit v7 on v5

--- a/solution.py
+++ b/solution.py
@@ -132,7 +132,7 @@
             copy.start()
             second.append(copy)
     for copy in second:
-        copy.wait()
+        copy.wait_recv()
     picked = far[owner_z]
     mine[...] = picked
     full[x // 2, :, :, lanes(x, z)] = picked
@@ -146,7 +146,7 @@
     fourth = []
     for j in (0, 1, 3, 2):
         if j:
-            third[j].wait()
+            third[j].wait_recv()
         s = (z + SIDE - j) % SIDE
         part = full.at[x // 2, :, :, lanes(x, s)]
         for k in (2, 1, 3):
@@ -157,6 +157,8 @@
             fourth.append(copy)
     for copy in fourth:
         copy.wait()
+    for copy in second + list(third.values()):
+        copy.wait_send()
     out_ref[...] = full[...]
 
 
@@ -472,8 +474,6 @@
     width = PAIRS // devices
     for g in range(devices):
         parts[g] = value[g * width : (g + 1) * width]
-    for copy in started:
-        copy.wait_send()
     moves = []
     for k in range(1, devices):
         peer = (me + k) % devices
@@ -485,6 +485,8 @@
     result = parts[me]
     for copy in moves:
         copy.wait()
+    for copy in started:
+        copy.wait_send()
     for k in range(1, devices):
         result = result + arrived[k]
     out_ref[...] = result

time: 113 us -> 113 us (level)
  no operation moved by 1% of the time
where the time goes in v7:
time: 113 us
  Pallas kernels  112 us (99%)
  local copies, waits for them, and re-layouts  1.23 us (1%)
    pallas_call x1, Pallas kernels, tail(): pl.pallas_call(functools.partial(tail_kernel, devices), out_shape=jax.Sha...  39.2 us
    pallas_call x1, Pallas kernels, spread(): pl.pallas_call(spread_kernel, out_shape=jax.ShapeDtypeStruct(whole, jnp.b...  37.2 us
    pallas_call x1, Pallas kernels, densities(): pl.pallas_call(functools.partial(density_kernel, devices), out_shape=[jax...  35.3 us

profile of v7, /device:TPU:1, one launch (start us, length us, event | category | flops | bytes accessed | tf_op | source)
XLA Modules:
  0.0 113.0 jit_solution(11994006600325810775)
XLA Ops:
  0.0 37.2 %spread_blocks.1.chosen = bf16[2,3,8,9216]{3,2,1,0:T(8,128)(2,1)} custom-call(s32[2]{0:T(128)} %blocks_ref.1, bf16[3,2,8,9216]{3,2,1,0:T(8,128)(2,1)} %bitcast.6), custom_call_target="tpu_custom_call" | custom-call | tf_op jit(solution)/shard_map/spread_blocks/pallas_call | solution.py:171
  37.2 35.3 %density_and_exchange.1 = (bf16[32,3,18,2,128]{4,3,2,1,0:T(2,128)(2,1)}, s32[1,192]{1,0:T(1,128)}) custom-call(bf16[2,3,8,9216]{3,2,1,0:T(8,128)(2,1)} %spread_blocks.1.chosen, bf16[3,8,9216]{2,1,0:T(8,128)(2,1)} %bitcast.7, bf16[136,384]{1,0:T(8,128)(2,1)} %constant.6.clone.z_mat, bf16[66,192]{1,0:T(8,128)(2,1)} %constant.7.clone.mix, s32[1,192]{1,0:T(1,128)} %bitcast.8), custom_call_target="tpu_custom_call" | custom-call | tf_op jit(solution)/shard_map/density_and_exchange/pallas_call | solution.py:298
  72.6 39.2 %screen_and_sum.1 = f32[2,64]{1,0:T(2,128)} custom-call(bf16[32,3,18,2,128]{4,3,2,1,0:T(2,128)(2,1)} %get-tuple-element.7.moved, bf16[96,192]{1,0:T(8,128)(2,1)} %constant.8.clone.mix, s32[1,192]{1,0:T(1,128)} %bitcast.9, s32[1,192]{1,0:T(1,128)} %get-tuple-element.8.twin_points, bf16[192,6144]{1,0:T(8,128)(2,1)} %screened.1), custom_call_target="tpu_custom_call" | custom-call | tf_op jit(solution)/shard_map/screen_and_sum/pallas_call | solution.py:502
  111.8 1.2 %copy.10 = f32[1,2,64]{2,1,0:T(2,128)} copy(f32[1,2,64]{2,1,0:T(2,128)} %bitcast.10) | data formatting | bytes 1024
